TPU v7x, 128 devices: a whole 4x4x4 slice. The times are simulated.
128 devices in a mesh: tm: 32 (over z, y, core), rows: 4 (over x).
Axes of the slice: x: 4, y: 4, z: 4, core: 2. Of those that a mesh axis runs over, the one named last changes fastest.
Arguments:
- covars: bfloat16 [524288, 128], P(('tm', 'rows')), may hold values from -5 to 5
- strata: int32 [524288], P(('tm', 'rows')), may hold values from 0 to 511
- centers: int32 [524288], P(('tm', 'rows')), may hold values from 0 to 2047
- events: int32 [524288], P(('tm', 'rows')), may hold values 0 or 1
- counts: int32 [128], P(('tm', 'rows')), may hold values from 1024 to 4096, as said below
- beta: float32 [128], replicated, may hold values from -0.4 to 0.4
- frailty: float32 [2048], replicated, may hold values from -3 to 3
Outputs:
- score: float32 [128], replicated
- info: float32 [128, 128], replicated
- center_score: float32 [2048], P(('tm', 'rows'))
- center_info: float32 [2048], P(('tm', 'rows'))
- center_cross: float32 [2048, 128], P(('tm', 'rows'))
Inputs may be any that keep to these rules, and one draw needn't show every extreme that they name: `counts`: each shard's live records come first; some shard is full.
All inputs are finite; a program needn't handle non-finite values. No bound on the sum of `events` on one device may be relied on, other than what follows from the above.
Results may differ from a plain program's by a relative error of at most 0.00067.
Values sent between devices are 32-bit elements; how exact they have to be, the bound alone decides.
No kernel may reach another device: no remote copies, remote signals or barrier semaphores. Data moves between devices by JAX's collectives and lax.ppermute only.
A program may use at most 64 MiB of HBM per device.

v0:
```python
import math

import jax
import jax.numpy as jnp
from jax import lax
from jax.sharding import PartitionSpec as P

STRATA = 512
CENTERS_DEV = 16


def prefix(value, axis, join, neutral, backward):
    count, mine = (lax.axis_size(axis), lax.axis_index(axis))
    pieces = jax.tree.map(lambda part: lax.all_gather(part, axis), value)
    if backward:
        pieces = jax.tree.map(lambda part: part[::-1], pieces)
        mine = count - 1 - mine
    so_far = jax.tree.map(
        lambda part, zero: jnp.full_like(part, 0) + jnp.asarray(zero, part.dtype), value, neutral
    )

    def lap(position, so_far):
        longer = join(so_far, jax.tree.map(lambda part: part[position], pieces))
        return jax.tree.map(lambda new, old: jnp.where(position < mine, new, old), longer, so_far)

    return lax.fori_loop(0, count - 1, lap, so_far)


def add_pairs(earlier, later):
    return (earlier[0] + later[0], earlier[1] + later[1])


def add_single(earlier, later):
    return earlier + later


def block_suffix(group_ids, weights, weighted, groups):
    record_count = group_ids.shape[0]
    block_size = min(512, record_count)
    blocks = record_count // block_size
    positions = jnp.arange(block_size)
    upper = positions[None, :] >= positions[:, None]
    labels = jnp.arange(groups)
    contract = (((0,), (0,)), ((), ()))

    def advance(carry, item):
        carry_zero, carry_one = carry
        block_ids, block_weights, block_rows = item
        shared = (block_ids[:, None] == block_ids[None, :]) & upper
        local_one = jnp.dot(
            shared.astype(jnp.bfloat16), block_rows, preferred_element_type=jnp.float32
        )
        local_zero = jnp.dot(
            shared.astype(jnp.float32), block_weights, precision=lax.Precision.HIGHEST
        )
        result = (local_zero + carry_zero[block_ids], local_one + carry_one[block_ids])
        member = block_ids[:, None] == labels[None, :]
        carry_one = carry_one + lax.dot_general(
            member.astype(jnp.bfloat16), block_rows, contract, preferred_element_type=jnp.float32
        )
        carry_zero = carry_zero + jnp.dot(
            block_weights, member.astype(jnp.float32), precision=lax.Precision.HIGHEST
        )
        return ((carry_zero, carry_one), result)

    init = (jnp.zeros((groups,), jnp.float32), jnp.zeros((groups, weighted.shape[1]), jnp.float32))
    items = (
        group_ids.reshape(blocks, block_size),
        weights.reshape(blocks, block_size),
        weighted.reshape(blocks, block_size, weighted.shape[1]),
    )
    totals, outputs = lax.scan(advance, init, items, reverse=True)
    return (
        outputs[0].reshape(record_count),
        outputs[1].reshape(record_count, weighted.shape[1]),
        totals,
    )


def block_prefix(group_ids, increments, groups):
    record_count = group_ids.shape[0]
    block_size = min(512, record_count)
    blocks = record_count // block_size
    positions = jnp.arange(block_size)
    lower = positions[None, :] <= positions[:, None]
    labels = jnp.arange(groups)

    def advance(carry, item):
        block_ids, block_incr = item
        shared = ((block_ids[:, None] == block_ids[None, :]) & lower).astype(jnp.float32)
        result = jnp.dot(shared, block_incr, precision=lax.Precision.HIGHEST) + carry[block_ids]
        member = (block_ids[:, None] == labels[None, :]).astype(jnp.float32)
        return (carry + jnp.dot(block_incr, member, precision=lax.Precision.HIGHEST), result)

    totals, outputs = lax.scan(
        advance,
        jnp.zeros((groups,), jnp.float32),
        (group_ids.reshape(blocks, block_size), increments.reshape(blocks, block_size)),
    )
    return (outputs.reshape(record_count), totals)


def later_moments(totals):
    empty = (jnp.zeros_like(totals[0]), jnp.zeros_like(totals[1]))
    shard_zero, shard_one = lax.psum((totals[0], totals[1]), "rows")
    outer = prefix((shard_zero, shard_one), "tm", add_pairs, empty, True)
    inner = prefix((totals[0], totals[1]), "rows", add_pairs, empty, True)
    return add_pairs(outer, inner)


def earlier_hazard(totals):
    empty = jnp.zeros_like(totals)
    shard_sum = lax.psum(totals, "rows")
    outer = prefix(shard_sum, "tm", add_single, empty, False)
    inner = prefix(totals, "rows", add_single, empty, False)
    return outer + inner


def body(covars, strata, centers, events, counts, beta, frailty):
    record_count = covars.shape[0]
    width = covars.shape[1]
    contract = (((0,), (0,)), ((), ()))
    live = jnp.arange(record_count) < counts[0]
    eta = (
        jnp.dot(covars, beta, precision=lax.Precision.HIGHEST, preferred_element_type=jnp.float32)
        + frailty[centers]
    )
    weights = jnp.where(live, jnp.exp(eta), 0.0)
    weighted = (weights[:, None] * covars.astype(jnp.float32)).astype(jnp.bfloat16)
    suffix_zero, suffix_one, totals = block_suffix(strata, weights, weighted, STRATA)
    later_zero, later_one = later_moments(totals)
    suffix_zero = suffix_zero + later_zero[strata]
    suffix_one = suffix_one + later_one[strata]
    flags = jnp.where(live, events, 0).astype(jnp.float32)
    safe_zero = jnp.where(flags > 0, suffix_zero, 1.0)
    increments = jnp.where(flags > 0, flags / safe_zero, 0.0)
    local_hazard, hazard_totals = block_prefix(strata, increments, STRATA)
    hazard = local_hazard + earlier_hazard(hazard_totals)[strata]
    exposure = weights * hazard
    mean_rows = jnp.where(flags[:, None] > 0, suffix_one / safe_zero[:, None], 0.0)
    mean_low = mean_rows.astype(jnp.bfloat16)
    loaded = (exposure[:, None] * covars.astype(jnp.float32)).astype(jnp.bfloat16)
    gradient = jnp.dot(
        flags.astype(jnp.bfloat16), covars, preferred_element_type=jnp.float32
    ) - jnp.sum(mean_rows, axis=0)
    curvature = lax.dot_general(
        covars, loaded, contract, preferred_element_type=jnp.float32
    ) - lax.dot_general(mean_low, mean_low, contract, preferred_element_type=jnp.float32)
    gradient, curvature = lax.psum((gradient, curvature), ("tm", "rows"))
    devices = lax.axis_size("tm") * lax.axis_size("rows")
    total = record_count * devices
    score = gradient / math.sqrt(total)
    info = curvature / total
    center_total = CENTERS_DEV * devices
    pair = jnp.stack(
        [
            jax.ops.segment_sum(flags - exposure, centers, num_segments=center_total),
            jax.ops.segment_sum(exposure, centers, num_segments=center_total),
        ]
    )
    block_size = min(2048, record_count)
    blocks = record_count // block_size
    labels = jnp.arange(center_total)

    def collect(accum, item):
        block_ids, block_rows = item
        member = (block_ids[:, None] == labels[None, :]).astype(jnp.bfloat16)
        return (
            accum
            + lax.dot_general(member, block_rows, contract, preferred_element_type=jnp.float32),
            None,
        )

    cross, unused_out = lax.scan(
        collect,
        jnp.zeros((center_total, width), jnp.float32),
        (centers.reshape(blocks, block_size), loaded.reshape(blocks, block_size, width)),
    )
    cross_mine, pair_mine = (
        lax.psum_scatter(cross, ("tm", "rows"), scatter_dimension=0, tiled=True),
        lax.psum_scatter(pair, ("tm", "rows"), scatter_dimension=1, tiled=True),
    )
    load = record_count // CENTERS_DEV
    root = math.sqrt(load)
    frailty_mine = lax.dynamic_slice_in_dim(
        frailty, lax.axis_index(("tm", "rows")) * CENTERS_DEV, CENTERS_DEV
    )
    center_score = pair_mine[0] / root - 0.5 * frailty_mine
    center_info = pair_mine[1] / load + 0.5
    center_cross = cross_mine / root
    return (score, info, center_score, center_info, center_cross)


def solution(mesh):
    in_specs = (
        P(("tm", "rows"), None),
        P(("tm", "rows")),
        P(("tm", "rows")),
        P(("tm", "rows")),
        P(("tm", "rows")),
        P(),
        P(),
    )
    out_specs = (P(), P(), P(("tm", "rows")), P(("tm", "rows")), P(("tm", "rows"), None))
    return jax.shard_map(body, mesh=mesh, in_specs=in_specs, out_specs=out_specs, check_vma=False)
```

profile of v0, /device:TPU:0, one launch (start us, length us, event | category | flops | bytes accessed | tf_op | source)
XLA Modules:
  0.0 1883.2 jit_solution(13553118793809692957)
XLA Ops:
  8.6 23.0 %gather_fusion.3 = f32[4096]{0:T(1024)S(1)} fusion(f32[2048]{0:T(1024)S(1)} %copy-done.1, s32[4096]{0:T(1024)S(1)} %fusion.55), kind=kCustom, calls=%fused_computation.3 | custom fusion | bytes 49152 | tf_op jit(solution)/shard_map/gather | solution.py:126
  34.9 58.8 %while.105 = (s32[]{:T(128)}, f32[512]{0:T(512)S(1)}, f32[512,128]{1,0:T(8,128)S(1)}, f32[8,512]{1,0:T(8,128)S(1)}, f32[8,512,128]{2,1,0:T(8,128)}, /*index=5*/f...) while((s32[]{:T(128)}, f32[512]{0:T(512)S(1)}, ...), condition=%wide.region_1.2_spmd.clone, body=%wide.region_0.1_spmd.clone.sunk | while | flops 142807040 | bytes 2419864 | solution.py:72
  94.5 26.7 %all-gather.12.cloned.1.call-done = f32[2048,128]{1,0:T(8,128)} async-done(((f32[512,128]{1,0:T(8,128)}), f32[2048,128]{1,0:T(8,128)}) %all-gather.12.cloned.1.call-update) | async-done | bytes 1048592 | tf_op jit(solution)/shard_map/all_gather | solution.py:14
  122.0 44.5 %all-reduce.3.cloned.1.call-done = f32[1,512,128]{2,1,0:T(8,128)} async-done(((f32[1,512,128]{2,1,0:T(8,128)}), f32[1,512,128]{2,1,0:T(8,128)}) %all-reduce.3.cloned.1.call-update) | async-done | bytes 262160 | tf_op jit(solution)/shard_map/psum | solution.py:105
  166.6 9.3 psum.35
  176.0 24.5 %all-gather.3 = f32[32,1,512]{2,1,0:T(1,128)S(1)} all-gather(f32[1,1,512]{2,1,0:T(1,128)S(1)} %bitcast.202), channel_id=1, replica_groups=mesh['tm'=32,'rows'=4] {'tm'}, dimensions={0}, use_global_device_ids=true | all-gather | bytes 67584 | tf_op jit(solution)/shard_map/all_gather | solution.py:14
  200.5 10.4 all-gather.4
  212.9 9.2 all-gather.10.cloned.1.call-done
  222.1 7.5 rev.13
  229.7 33.7 %while.106 = (s32[]{:T(128)}, f32[512]{0:T(512)S(1)}, f32[512,128]{1,0:T(8,128)S(1)}, s32[]{:T(128)}, f32[32,512]{1,0:T(8,128)S(1)}, /*index=5*/f32[32,512,128]{2,1,0:T(8,128)}, s32[]{:T(128)}, s32[]{:T(128)}) while((s32[]{:T(128)}, f32[512]{0:T(512)S(1)}, f32[512,128]{1,0:T(8,128)S(1)}, s32[]{:T(128)}, f32[32,512]{1,0:T(8,128)S(1)}, ...), condition=%wide.region_5.6_spmd.clone, body=%wide.region_4.5_spmd.clone.sunk | while | flops 198148 | bytes 796787 | solution.py:26
  263.4 25.9 %gather_fusion.5 = f32[4096]{0:T(1024)S(1)} fusion(f32[512]{0:T(512)S(1)} %add.293, s32[4096]{0:T(1024)S(1)} %fusion.56), kind=kCustom, calls=%fused_computation.5 | custom fusion | bytes 49152 | tf_op jit(solution)/shard_map/gather | solution.py:132
  289.4 37.0 %while.108 = (s32[]{:T(128)}, f32[512]{0:T(512)S(1)}, f32[8,512]{1,0:T(8,128)S(1)}, f32[8,512]{1,0:T(8,128)S(1)}, s32[8,512]{1,0:T(8,128)S(1)}, /*index=5*/s32[]{:T(128)}, s32[]{:T(128)}) while((s32[]{:T(128)}, f32[512]{0:T(512)S(1)}, f32[8,512]{1,0:T(8,128)S(1)}, f32[8,512]{1,0:T(8,128)S(1)}, s32[8,512]{1,0:T(8,128)S(1)}, ...), condition=%wide.region_11.12_spmd.clone, body=%wide.region_10.11_spmd.clone.sunk | while | flops 7344131 | bytes 51303 | solution.py:95
  326.5 10.4 psum.38
  336.9 23.9 %all-gather.5 = f32[32,1,512]{2,1,0:T(1,128)S(1)} all-gather(f32[1,1,512]{2,1,0:T(1,128)S(1)} %bitcast.203), channel_id=1, replica_groups=mesh['tm'=32,'rows'=4] {'tm'}, dimensions={0}, use_global_device_ids=true | all-gather | bytes 67584 | tf_op jit(solution)/shard_map/all_gather | solution.py:14
  362.5 10.4 all-gather.6
  373.1 25.9 %gather_fusion.6 = f32[4096]{0:T(1024)S(1)} fusion(f32[512]{0:T(512)S(1)} %add.295, s32[4096]{0:T(1024)S(1)} %fusion.56), kind=kCustom, calls=%fused_computation.6 | custom fusion | bytes 49152 | tf_op jit(solution)/shard_map/gather | solution.py:138
  401.7 22.0 %scatter_custom_fusion.1 = f32[2048]{0:T(1024)S(1)} fusion(s32[4096]{0:T(1024)S(1)} %copy-done.7, f32[4096]{0:T(1024)S(1)} %get-tuple-element.902, f32[]{:T(128)} %constant.197.clone.1), kind=kCustom, calls=%fused_computation.112 | custom fusion | flops 4096 | bytes 8196 | tf_op jit(solution)/shard_map/scatter-add | solution.py:158
  423.8 14.2 gather_fusion.4
  445.3 22.0 %scatter_custom_fusion = f32[2048]{0:T(1024)S(1)} fusion(s32[4096]{0:T(1024)S(1)} %copy-done.7, f32[4096]{0:T(1024)S(1)} %get-tuple-element.901, f32[]{:T(128)} %constant.197.clone.1), kind=kCustom, calls=%fused_computation.114 | custom fusion | flops 4096 | bytes 8196 | tf_op jit(solution)/shard_map/scatter-add | solution.py:157
  468.8 14.2 while.111
  486.6 62.9 %psum.37 = f32[128]{0:T(128)S(1)} all-reduce(f32[128]{0:T(128)S(1)} %fusion.53), channel_id=1, replica_groups=mesh['tm'=32,'rows'=4] {'tm','rows'}, use_global_device_ids=true, to_apply=%region_9.10 | all-reduce | flops 128 | bytes 1024 | tf_op jit(solution)/shard_map/psum | solution.py:149
  550.0 30.6 %all-reduce.5.cloned.1.call-done = f32[128,128]{0,1:T(8,128)} async-done(((f32[128,128]{0,1:T(8,128)}), f32[128,128]{0,1:T(8,128)}) %all-reduce.5.cloned.1.call-update) | async-done | bytes 65552 | tf_op jit(solution)/shard_map/psum | solution.py:149
  582.2 648.3 %reduce-scatter.7.cloned.1.call-done = f32[16,2]{1,0:T(8,128)} async-done(((f32[2048,2]{1,0:T(8,128)}), f32[16,2]{1,0:T(8,128)}) %reduce-scatter.7.cloned.1.call-update) | async-done | bytes 144
  1232.6 642.5 %reduce-scatter.5.cloned.1.call-done = f32[16,128]{1,0:T(8,128)} async-done(((f32[2048,128]{1,0:T(8,128)}), f32[16,128]{1,0:T(8,128)}) %reduce-scatter.5.cloned.1.call-update) | async-done | bytes 8208 | tf_op jit(solution)/shard_map/reduce_scatter | solution.py:180
  (420 shorter events, 172.6 us)
Async XLA Ops:
  7.2 24.5 %copy-start = (f32[128]{0:T(128)S(1)}, f32[128]{0:T(128)}, u32[]{:S(2)}) copy-start(f32[128]{0:T(128)} %param.26) | copy-start | bytes 1540
  7.2 1.4 copy-start.1
  7.2 114.0 %all-gather.12.cloned.1.call-start = ((), (), s32[]{:S(2)}) async-start(), calls=%async_computation.6 | async-start | bytes 1310720 | tf_op jit(solution)/shard_map/all_gather | solution.py:14
  8.6 23.1 %copy-start.2 = (bf16[4096,128]{1,0:T(8,128)(2,1)S(1)}, bf16[4096,128]{1,0:T(8,128)(2,1)}, u32[]{:S(2)}) copy-start(bf16[4096,128]{1,0:T(8,128)(2,1)} %param.21) | copy-start | bytes 3145732
  31.7 1.7 copy-start.6
  34.9 131.7 %copy-start.7 = (s32[4096]{0:T(1024)S(1)}, s32[4096]{0:T(1024)}, u32[]{:S(2)}) copy-start(s32[4096]{0:T(1024)} %param.23) | copy-start | bytes 49156
  93.7 0.7 copy-start.3
  121.2 45.3 %all-reduce.3.cloned.1.call-start = ((), (), s32[]{:S(2)}) async-start(), calls=%async_computation.2 | async-start | bytes 524288 | tf_op jit(solution)/shard_map/psum | solution.py:105
  121.9 100.2 %all-gather.10.cloned.1.call-start = ((), (), s32[]{:S(2)}) async-start(), calls=%async_computation.3 | async-start | bytes 8650752 | tf_op jit(solution)/shard_map/all_gather | solution.py:14
  166.5 414.1 %all-reduce.5.cloned.1.call-start = ((), (), s32[]{:S(2)}) async-start(), calls=%async_computation.4 | async-start | bytes 131072 | tf_op jit(solution)/shard_map/psum | solution.py:149
  263.4 26.0 %copy-start.5 = (s32[4096]{0:T(1024)S(1)}, s32[4096]{0:T(1024)}, u32[]{:S(2)}) copy-start(s32[4096]{0:T(1024)} %param.24) | copy-start | bytes 49156
  445.1 785.4 %reduce-scatter.7.cloned.1.call-start = ((), (), s32[]{:S(2)}) async-start(), calls=%async_computation.7 | async-start | bytes 1056768
  468.8 1406.3 %reduce-scatter.5.cloned.1.call-start = ((), (), s32[]{:S(2)}) async-start(), calls=%async_computation.5 | async-start | bytes 1056768 | tf_op jit(solution)/shard_map/reduce_scatter | solution.py:180
  468.8 14.3 copy-start.4
Sparse Core Ops, SparseCore 0:
  94.6 26.5 all-gather.11
  124.3 42.1 all-reduce.2
  168.7 53.3 all-gather.9
  445.2 135.3 all-reduce.4
  582.8 647.6 reduce-scatter.6
  1232.7 642.3 reduce-scatter.4
where the time goes:
time: 1880 us
  waiting for transfers between devices  1400 us (74%)
  local copies, waits for them, and re-layouts  170 us (9%)
  blocking collectives  152 us (8%)
  other arithmetic  88.1 us (5%)
  matrix products  52 us (3%)
    unnamed x7, waiting for transfers between devices  649 us
    reduce_scatter x1, waiting for transfers between devices, body(): lax.psum_scatter(cross, ('tm', 'rows'), scatter_dimension=0, tiled=True)  642 us
    all_gather x4, blocking collectives, prefix(): pieces = jax.tree.map(lambda part: lax.all_gather(part, axis), value)  69.2 us
    psum x1, blocking collectives, body(): gradient, curvature = lax.psum((gradient, curvature), ('tm', 'rows'))  62.9 us
    psum x1, waiting for transfers between devices, later_moments(): shard_zero, shard_one = lax.psum((totals[0], totals[1]), 'rows')  44.5 us
  transfers between devices with their start and end apart: 6, of which 6 were waited for; matrix products, arithmetic and copies ran while one was open for 3% of the time, Pallas kernels for 0%

commit v1 on v0

v1 whole, which is shorter than its diff:
```python
import math

import jax
import jax.numpy as jnp
from jax import lax
from jax.experimental import pallas as pl
from jax.experimental.pallas import tpu as pltpu
from jax.sharding import PartitionSpec as P

STRATA = 512
CENTERS_DEV = 16
AXES = ("tm", "rows")
BLOCK = 512
LANES = 128
F32 = jnp.float32
BF16 = jnp.bfloat16
NN = (((1,), (0,)), ((), ()))
NT = (((1,), (1,)), ((), ()))
TN = (((0,), (0,)), ((), ()))


def mxu(left, right, dims=NN):
    return lax.dot_general(left, right, dims, preferred_element_type=F32)


def iota(shape, dim):
    return lax.broadcasted_iota(jnp.int32, shape, dim)


def split3(value):
    high = value.astype(BF16).astype(F32)
    rest = value - high
    middle = rest.astype(BF16).astype(F32)
    return high, middle, (rest - middle).astype(BF16).astype(F32)


def stack(rows, height):
    at = iota((height, rows[0].shape[1]), 0)
    out = jnp.zeros(at.shape, F32)
    for place, row in enumerate(rows):
        out = jnp.where(at == place, row, out)
    return out.astype(BF16)


def one_hot(ids, height):
    return jnp.where(iota((height, ids.shape[1]), 0) == ids, 1.0, 0.0).astype(BF16)


def columns(rows, width=LANES):
    return mxu(stack(rows, 8), jnp.ones((8, width), BF16), TN)


def table_rows(table):
    return jnp.concatenate(split3(table), axis=0).astype(BF16)


def look_up(rows, upper, lower_hot, height):
    picked = mxu(rows, lower_hot)
    picked = picked[:height] + picked[height : 2 * height] + picked[2 * height :]
    hit = iota(picked.shape, 0) == upper
    return jnp.sum(jnp.where(hit, picked, 0.0), axis=0, keepdims=True)


def add_up(values, upper, lower_hot, height):
    at = iota((height, values.shape[1]), 0)
    parts = [jnp.where(at == upper, part, 0.0) for part in split3(values)]
    sums = mxu(jnp.concatenate(parts, axis=0).astype(BF16), lower_hot, NT)
    return sums[:height] + sums[height : 2 * height] + sums[2 * height :]


def id_columns(ids):
    upper = ids & ~255
    column = columns([upper.astype(F32), (ids - upper).astype(F32)])
    return jnp.concatenate([column] * (STRATA // LANES), axis=1)


def same_and_later(ids, id_column):
    square = (BLOCK, BLOCK)
    later = iota(square, 1) >= iota(square, 0)
    return jnp.where((id_column == ids.astype(F32)) & later, 1.0, 0.0).astype(BF16)


def members(id_column):
    labels = iota((BLOCK, STRATA), 1).astype(F32)
    return jnp.where(id_column == labels, 1.0, 0.0).astype(BF16)


def strided(start, count):
    return pl.ds(start, count, stride=8)


def weigh_kernel(counts, strata, centers, covars, beta, frailty, w_out, wx_out, send):
    records = covars.shape[0]
    betas = stack(split3(beta[...]), 8)
    table = table_rows(frailty[...])
    total_zero = jnp.zeros((8, LANES), F32)
    total_one = jnp.zeros((STRATA, LANES), F32)
    for start in range(0, records, BLOCK):
        span = pl.ds(start, BLOCK)
        ids, owners, rows = strata[:, span], centers[:, span], covars[span, :]
        eta = jnp.sum(mxu(betas, rows, NT), axis=0, keepdims=True) + look_up(
            table, owners >> 7, one_hot(owners & 127, LANES), frailty.shape[0]
        )
        live = iota((1, BLOCK), 1) + start < counts[0]
        weight = jnp.where(live, jnp.exp(eta), 0.0)
        w_out[:, span] = weight
        weighted = (columns(split3(weight)) * rows.astype(F32)).astype(BF16)
        wx_out[span, :] = weighted
        total_one = total_one + mxu(one_hot(ids, STRATA), weighted)
        total_zero = total_zero + add_up(weight, ids >> 7, one_hot(ids & 127, LANES), 8)
    devices = send.shape[0] // 8
    for place in range(4):
        send[strided(place, devices), :] = jnp.broadcast_to(
            total_zero[place : place + 1], (devices, LANES)
        )
        send[strided(4 + place, devices), :] = total_one[place * LANES : (place + 1) * LANES]


def suffix_kernel(strata, w_in, wx_in, zero_out, one_out):
    records = wx_in.shape[0]
    carry_zero = jnp.zeros((8, LANES), F32)
    carry_one = jnp.zeros((STRATA, LANES), F32)
    for start in reversed(range(0, records, BLOCK)):
        span = pl.ds(start, BLOCK)
        ids, weight, weighted = strata[:, span], w_in[:, span], wx_in[span, :]
        id_column = id_columns(ids)
        shared = same_and_later(ids, id_column)
        lower_hot = one_hot(ids & 127, LANES)
        zero = jnp.sum(mxu(stack(split3(weight), 8), shared, NT), axis=0, keepdims=True)
        zero_out[:, span] = zero + look_up(table_rows(carry_zero), ids >> 7, lower_hot, 8)
        high = carry_one.astype(BF16)
        low = (carry_one - high.astype(F32)).astype(BF16)
        later = mxu(members(id_column), jnp.concatenate([high, low], axis=1))
        one_out[span, :] = mxu(shared, weighted) + later[:, :LANES] + later[:, LANES:]
        carry_one = carry_one + mxu(one_hot(ids, STRATA), weighted)
        carry_zero = carry_zero + add_up(weight, ids >> 7, lower_hot, 8)


def hazard_kernel(counts, mine, strata, events, zero_in, received, q_out, send, later):
    records = strata.shape[1]
    devices = received.shape[0] // 8
    running = jnp.zeros((8, LANES), F32)
    for device in reversed(range(devices)):
        slab = pl.ds(device * 8, 8)
        later[slab, :] = running
        running = running + received[slab, :]
    table = table_rows(later[pl.ds(pl.multiple_of(mine[0] * 8, 8), 8), :])
    total = jnp.zeros((8, LANES), F32)
    for start in range(0, records, BLOCK):
        span = pl.ds(start, BLOCK)
        ids = strata[:, span]
        lower_hot = one_hot(ids & 127, LANES)
        zero = zero_in[:, span] + look_up(table, ids >> 7, lower_hot, 8)
        live = iota((1, BLOCK), 1) + start < counts[0]
        happened = live & (events[:, span] > 0)
        increment = jnp.where(happened, 1.0 / jnp.where(happened, zero, 1.0), 0.0)
        q_out[:, span] = increment
        total = total + add_up(increment, ids >> 7, lower_hot, 8)
    mask = iota((8, LANES), 0) < 4
    for device in range(devices):
        slab = pl.ds(device * 8, 8)
        send[slab, :] = jnp.where(mask, total, later[slab, :])


def prefix_kernel(strata, q_in, out):
    records = strata.shape[1]
    carry = jnp.zeros((8, LANES), F32)
    for start in range(0, records, BLOCK):
        span = pl.ds(start, BLOCK)
        ids, increment = strata[:, span], q_in[:, span]
        shared = same_and_later(ids, id_columns(ids))
        lower_hot = one_hot(ids & 127, LANES)
        local = jnp.sum(mxu(stack(split3(increment), 8), shared), axis=0, keepdims=True)
        out[:, span] = local + look_up(table_rows(carry), ids >> 7, lower_hot, 8)
        carry = carry + add_up(increment, ids >> 7, lower_hot, 8)


def moments_kernel(
    counts, mine, strata, centers, events, w_in, q_in, hazard_in, covars, one_in, received,
    loaded_out, pack,
):
    records, width = covars.shape
    devices = received.shape[0] // 8
    before = (iota((devices * 8, LANES), 0) >> 3) < mine[0]
    earlier = jnp.where(before, received[...], 0.0).reshape(devices, 8, LANES).sum(axis=0)
    table = table_rows(earlier)
    later = jnp.concatenate([received[strided(4 + r, devices), :] for r in range(4)], axis=0)
    high = later.astype(BF16)
    low = (later - high.astype(F32)).astype(BF16)
    later = jnp.concatenate([high, low], axis=1)
    sixteen = iota((16, 2 * LANES), 0)
    left = iota((16, 2 * LANES), 1) < LANES
    spread = jnp.where(
        (left & (sixteen < 3)) | (~left & (sixteen >= 3) & (sixteen < 6)), 1.0, 0.0
    ).astype(BF16)
    groups = 16
    pairs = jnp.zeros((4 * groups, LANES), F32)
    curvature = jnp.zeros((width, width), F32)
    gradient = jnp.zeros((1, width), F32)
    for start in range(0, records, BLOCK):
        span = pl.ds(start, BLOCK)
        ids, owners, rows = strata[:, span], centers[:, span], covars[span, :]
        increment = q_in[:, span]
        hazard = hazard_in[:, span] + look_up(table, ids >> 7, one_hot(ids & 127, LANES), 8)
        exposure = w_in[:, span] * hazard
        live = iota((1, BLOCK), 1) + start < counts[0]
        happened = jnp.where(live & (events[:, span] > 0), 1.0, 0.0)
        parts = split3(exposure)
        both = mxu(stack([*parts, *split3(increment)], 16), spread, TN)
        loaded = (both[:, :LANES] * rows.astype(F32)).astype(BF16)
        loaded_out[span, :] = loaded
        outside = mxu(members(id_columns(ids)), later)
        mean = (one_in[span, :] + outside[:, :LANES] + outside[:, LANES:]) * both[:, LANES:]
        mean_low = mean.astype(BF16)
        curvature = curvature + mxu(rows, loaded, TN) - mxu(mean_low, mean_low, TN)
        flags = mxu(stack([happened], 8), rows)
        gradient = gradient + flags[:1] - jnp.sum(mean, axis=0, keepdims=True)
        at = iota((groups, BLOCK), 0)
        chosen = [jnp.where(at == owners >> 7, part, 0.0) for part in (*parts, happened)]
        pairs = pairs + mxu(
            jnp.concatenate(chosen, axis=0).astype(BF16), one_hot(owners & 127, LANES), NT
        )
    exposed = pairs[:groups] + pairs[groups : 2 * groups] + pairs[2 * groups : 3 * groups]
    pack[0:width, :] = curvature
    pack[width : width + 8, :] = jnp.broadcast_to(gradient, (8, width))
    pack[width + 8 : width + 24, :] = pairs[3 * groups :] - exposed
    pack[width + 24 : width + 40, :] = exposed


def cross_kernel(centers, loaded, out):
    tile = 256
    for start in range(0, out.shape[0], tile):
        out[pl.ds(start, tile), :] = mxu(one_hot(centers[...] - start, tile), loaded[...])


def call(kernel, out_shape, scratch=(), scalars=0, **kwargs):
    def run(*args):
        specs = [
            pl.BlockSpec(memory_space=pltpu.SMEM if place < scalars else pltpu.VMEM)
            for place in range(len(args))
        ]
        return pl.pallas_call(
            kernel,
            out_shape=out_shape,
            in_specs=specs,
            out_specs=jax.tree.map(lambda _: pl.BlockSpec(memory_space=pltpu.VMEM), out_shape),
            scratch_shapes=list(scratch),
            name=kernel.__name__,
            **kwargs,
        )(*args)

    return run


def shaped(*shape, dtype=F32):
    return jax.ShapeDtypeStruct(shape, dtype)


def place_of(z, y, c, x):
    return ((z * 4 + y) * 2 + c) * 4 + x


def moves(step):
    grid = [
        (z, y, c, x) for z in range(4) for y in range(4) for c in range(2) for x in range(4)
    ]
    return [(place_of(*at), place_of(*step(*at))) for at in grid]


def sum_everywhere(value):
    value = value + lax.ppermute(value, AXES, moves(lambda z, y, c, x: (z, y, 1 - c, x)))
    rings = (
        lambda k: lambda z, y, c, x: (z, y, c, (x + k) % 4),
        lambda k: lambda z, y, c, x: (z, (y + k) % 4, c, x),
        lambda k: lambda z, y, c, x: ((z + k) % 4, y, c, x),
    )
    for ring in rings:
        others = [lax.ppermute(value, AXES, moves(ring(k))) for k in (1, 2, 3)]
        value = (value + others[1]) + (others[0] + others[2])
    return value


def exchange(value):
    devices = value.shape[0] // 8
    out = lax.all_to_all(value.reshape(devices, 8, LANES), AXES, 0, 0, tiled=True)
    return out.reshape(devices * 8, LANES)


def body(covars, strata, centers, events, counts, beta, frailty):
    records, width = covars.shape
    devices = lax.axis_size("tm") * lax.axis_size("rows")
    center_total = CENTERS_DEV * devices
    mine = lax.axis_index(AXES)
    me = mine.reshape(1).astype(jnp.int32)
    strata, centers, events = (part.reshape(1, records) for part in (strata, centers, events))
    slabs = shaped(devices * 8, LANES)
    line = shaped(1, records)
    weights, weighted, totals = call(
        weigh_kernel, (line, shaped(records, width, dtype=BF16), slabs), scalars=1
    )(counts, strata, centers, covars, beta.reshape(1, width), frailty.reshape(-1, LANES))
    received = exchange(totals)
    suffix_zero, suffix_one = call(suffix_kernel, (line, shaped(records, width)))(
        strata, weights, weighted
    )
    increments, send = call(
        hazard_kernel, (line, slabs), scratch=[pltpu.VMEM((devices * 8, LANES), F32)], scalars=2
    )(counts, me, strata, events, suffix_zero, received)
    arrived = exchange(send)
    local_hazard = call(prefix_kernel, line)(strata, increments)
    loaded, pack = call(
        moments_kernel,
        (shaped(records, width, dtype=BF16), shaped(width + 40, LANES)),
        scalars=2,
    )(
        counts, me, strata, centers, events, weights, increments, local_hazard, covars,
        suffix_one, arrived,
    )
    cross = call(cross_kernel, shaped(center_total, width))(centers, loaded)
    shares = lax.all_to_all(
        cross.reshape(devices, CENTERS_DEV, width), AXES, 0, 0, tiled=True
    )
    pack = sum_everywhere(pack)
    total = records * devices
    info = pack[:width] / total
    score = pack[width] / math.sqrt(total)
    load = records // CENTERS_DEV
    root = math.sqrt(load)
    pairs = pack[width + 8 :].reshape(2, center_total)
    first = mine * CENTERS_DEV
    pairs = lax.dynamic_slice_in_dim(pairs, first, CENTERS_DEV, axis=1)
    frailty_mine = lax.dynamic_slice_in_dim(frailty, first, CENTERS_DEV)
    center_score = pairs[0] / root - 0.5 * frailty_mine
    center_info = pairs[1] / load + 0.5
    center_cross = jnp.sum(shares, axis=0) / root
    return (score, info, center_score, center_info, center_cross)


def solution(mesh):
    in_specs = (
        P(AXES, None),
        P(AXES),
        P(AXES),
        P(AXES),
        P(AXES),
        P(),
        P(),
    )
    out_specs = (P(), P(), P(AXES), P(AXES), P(AXES, None))
    return jax.shard_map(body, mesh=mesh, in_specs=in_specs, out_specs=out_specs, check_vma=False)
```

time: 1880 us -> 120 us (0.06)
  waiting for transfers between devices: 1400 us -> 37.8 us
  local copies, waits for them, and re-layouts: 170 us -> 1.68 us
  blocking collectives: 152 us -> 0 us
  other arithmetic: 88.1 us -> 4.65 us
  matrix products: 52 us -> 0 us
  Pallas kernels: 0 us -> 36.4 us
  starting transfers between devices: 0.38 us -> 36.7 us
    unnamed x7 -> x0, waiting for transfers between devices: 649 us -> none
    reduce_scatter x1 -> x0, waiting for transfers between devices: 642 us -> none  [body(): lax.psum_scatter(cross, ('tm', 'rows'), scatter_dimension=0, tiled=True)]
    gather x28 -> x0, local copies, waits for them, and re-layouts: 153 us -> none  [the longest x8 28 us: advance(): carry[block_ids]]
    psum x3 -> x0, blocking collectives: 82.7 us -> none  [the longest x1 62.9 us: body(): gradient, curvature = lax.psum((gradient, curvature), ('tm', 'rows'))]
    psum x2 -> x0, waiting for transfers between devices: 75.1 us -> none  [the longest x1 44.5 us: later_moments(): shard_zero, shard_one = lax.psum((totals[0], totals[1]), 'rows')]
    all_gather x4 -> x0, blocking collectives: 69.2 us -> none  [prefix(): pieces = jax.tree.map(lambda part: lax.all_gather(part, axis), value)]
    dot_general x54 -> x0, matrix products: 52 us -> none  [the longest x2 14.2 us: collect(): lax.dot_general(member, block_rows, contract, preferred_element_type=jnp....]
    scatter-add x2 -> x0, other arithmetic: 44 us -> none  [the longest x1 22 us: body(): jax.ops.segment_sum(exposure, centers, num_segments=center_total)]
  transfers between devices with their start and end apart: 6 -> 13, of which waited for: 6 -> 8; matrix products, arithmetic and copies ran while one was open for 3% -> 3% of each run, Pallas kernels for 0% -> 16%
where the time goes in v1:
time: 120 us; the launch traced here: 119 us
  waiting for transfers between devices  37.8 us (31%)
  starting transfers between devices  36.7 us (31%)
  Pallas kernels  36.4 us (30%)
  other arithmetic  4.65 us (4%)
  local copies, waits for them, and re-layouts  1.68 us (1%)
  between operations  1.37 us (1%)
    pallas_call x6, Pallas kernels, run(): pl.pallas_call(kernel, out_shape=out_shape, in_specs=specs, out_specs=jax...  36.4 us
    all_to_all x2, starting transfers between devices, exchange(): lax.all_to_all(value.reshape(devices, 8, LANES), AXES, 0, 0, tiled=True)  16.5 us
    all_to_all x1, waiting for transfers between devices, body(): lax.all_to_all(cross.reshape(devices, CENTERS_DEV, width), AXES, 0, 0, ti...  15.7 us
    all_to_all x2, waiting for transfers between devices, exchange(): lax.all_to_all(value.reshape(devices, 8, LANES), AXES, 0, 0, tiled=True)  14.4 us
    ppermute x9, starting transfers between devices, sum_everywhere(): others = [lax.ppermute(value, AXES, moves(ring(k))) for k in (1, 2, 3)]  14.1 us
    ppermute x9, waiting for transfers between devices, sum_everywhere(): others = [lax.ppermute(value, AXES, moves(ring(k))) for k in (1, 2, 3)]  6.34 us
    all_to_all x1, starting transfers between devices, body(): lax.all_to_all(cross.reshape(devices, CENTERS_DEV, width), AXES, 0, 0, ti...  5.99 us
  transfers between devices with their start and end apart: 13, of which 8 were waited for; matrix products, arithmetic and copies ran while one was open for 3% of the time, Pallas kernels for 16%

profile of v1, /device:TPU:0, one launch (start us, length us, event | category | flops | bytes accessed | tf_op | source)
XLA Modules:
  0.0 118.6 jit_solution(1865856239317118835)
XLA Ops:
  1.3 5.9 %weigh_kernel.1 = (f32[1,4096]{1,0:T(1,128)}, bf16[4096,128]{1,0:T(8,128)(2,1)}, f32[1024,128]{1,0:T(8,128)}) custom-call(s32[1]{0:T(128)S(6)} %copy.12.counts, s32[1,4096]{1,0:T(1,128)} %bitcast.22, s32[1,4096]{1,0:T(1,128)} %bitcast.27, bf16[4096,128]{1,0:T(8,128)(2,1)} %covars.3, f32[1,128]{1,0:T(1,128)} %bitcast.33, f32[16,128]{1,0:T(8,128)} %bitcast.32), custom_call_target="tpu_custom_call" | custom-call | tf_op jit(solution)/shard_map/weigh_kernel/pallas_call | solution.py:242
  7.2 11.2 %all-to-all-start = ((f32[128,8,128]{2,1,0:T(8,128)}), f32[128,8,128]{2,1,0:T(8,128)S(1)}, u32[]{:S(2)}, u32[]{:S(2)}) async-start(f32[128,8,128]{2,1,0:T(8,128)} %bitcast.20), calls=%async_computation | async-start | bytes 1048576 | tf_op jit(solution)/shard_map/all_to_all | solution.py:285
  18.4 8.6 %suffix_kernel.1 = (f32[1,4096]{1,0:T(1,128)}, f32[4096,128]{1,0:T(8,128)}) custom-call(s32[1,4096]{1,0:T(1,128)} %bitcast.23, f32[1,4096]{1,0:T(1,128)} %get-tuple-element.14.w_in, bf16[4096,128]{1,0:T(8,128)(2,1)} %get-tuple-element.15.wx_in), custom_call_target="tpu_custom_call" | custom-call | tf_op jit(solution)/shard_map/suffix_kernel/pallas_call | solution.py:242
  26.9 4.7 %all-to-all-done = f32[128,8,128]{2,1,0:T(8,128)S(1)} async-done(((f32[128,8,128]{2,1,0:T(8,128)}), f32[128,8,128]{2,1,0:T(8,128)S(1)}, u32[]{:S(2)}, u32[]{:S(2)}) %all-to-all-start) | async-done | bytes 524320 | tf_op jit(solution)/shard_map/all_to_all | solution.py:285
  32.4 3.2 %hazard_kernel.1 = (f32[1,4096]{1,0:T(1,128)}, f32[1024,128]{1,0:T(8,128)}) custom-call(s32[1]{0:T(128)S(6)} %copy.12.counts, s32[1]{0:T(128)} %bitcast.mine, s32[1,4096]{1,0:T(1,128)} %bitcast.24, s32[1,4096]{1,0:T(1,128)} %bitcast.30, f32[1,4096]{1,0:T(1,128)} %get-tuple-element.16.zero_in, f32[1024,128]{1,0:T(8,128)} %bitcast.18), custom_call_target="tpu_custom_call" | custom-call | tf_op jit(solution)/shard_map/hazard_kernel/pallas_call | solution.py:242
  35.6 5.3 %all-to-all-start.1 = ((f32[128,8,128]{2,1,0:T(8,128)}), f32[128,8,128]{2,1,0:T(8,128)S(1)}, u32[]{:S(2)}, u32[]{:S(2)}) async-start(f32[128,8,128]{2,1,0:T(8,128)} %bitcast.21), calls=%async_computation.1 | async-start | bytes 1048576 | tf_op jit(solution)/shard_map/all_to_all | solution.py:285
  40.9 3.3 %prefix_kernel.1.hazard_in = f32[1,4096]{1,0:T(1,128)} custom-call(s32[1,4096]{1,0:T(1,128)} %bitcast.25, f32[1,4096]{1,0:T(1,128)} %get-tuple-element.18.q_in), custom_call_target="tpu_custom_call" | custom-call | tf_op jit(solution)/shard_map/prefix_kernel/pallas_call | solution.py:242
  44.1 9.8 %all-to-all-done.1 = f32[128,8,128]{2,1,0:T(8,128)S(1)} async-done(((f32[128,8,128]{2,1,0:T(8,128)}), f32[128,8,128]{2,1,0:T(8,128)S(1)}, u32[]{:S(2)}, u32[]{:S(2)}) %all-to-all-start.1) | async-done | bytes 524320 | tf_op jit(solution)/shard_map/all_to_all | solution.py:285
  54.7 8.8 %moments_kernel.1 = (bf16[4096,128]{1,0:T(8,128)(2,1)}, f32[168,128]{1,0:T(8,128)}) custom-call(s32[1]{0:T(128)S(6)} %copy.12.counts, s32[1]{0:T(128)} %bitcast.mine, s32[1,4096]{1,0:T(1,128)} %bitcast.26, s32[1,4096]{1,0:T(1,128)} %bitcast.28, s32[1,4096]{1,0:T(1,128)} %bitcast.31, f32[1,4096]{1,0:T(1,128)} %get-tuple-element.14.w_in, ...), custom_call_target="tpu_custom_call" | custom-call | tf_op jit(solution)/shard_map/moments_kernel/pallas_call | solution.py:242
  63.6 1.4 %collective-permute-done = f32[168,128]{1,0:T(8,128)S(1)} collective-permute-done((f32[168,128]{1,0:T(8,128)}, f32[168,128]{1,0:T(8,128)S(1)}, u32[]{:S(2)}, u32[]{:S(2)}) %collective-permute-start) | collective-permute-done | bytes 86048 | tf_op jit(solution)/shard_map/ppermute | solution.py:271
  65.9 1.5 %collective-permute-start.1 = (f32[168,128]{1,0:T(8,128)S(1)}, f32[168,128]{1,0:T(8,128)S(1)}, u32[]{:S(2)}, u32[]{:S(2)}) collective-permute-start(f32[168,128]{1,0:T(8,128)S(1)} %add.44), channel_id=1, source_target_pairs={{0,2},{1,3},{2,0},{3,1},{4,6},{5,7},{6,4},{7,5},{8,10},{9,11},{10,... | collective-permute-start | bytes 258056 | tf_op jit(solution)/shard_map/ppermute | solution.py:278
  68.3 2.3 %collective-permute-start.3 = (f32[168,128]{1,0:T(8,128)S(1)}, f32[168,128]{1,0:T(8,128)S(1)}, u32[]{:S(2)}, u32[]{:S(2)}) collective-permute-start(f32[168,128]{1,0:T(8,128)S(1)} %add.44), channel_id=1, source_target_pairs={{0,3},{1,0},{2,1},{3,2},{4,7},{5,4},{6,5},{7,6},{8,11},{9,8},{10,9... | collective-permute-start | bytes 258056 | tf_op jit(solution)/shard_map/ppermute | solution.py:278
  70.6 2.3 %collective-permute-done.1 = f32[168,128]{1,0:T(8,128)S(1)} collective-permute-done((f32[168,128]{1,0:T(8,128)S(1)}, f32[168,128]{1,0:T(8,128)S(1)}, u32[]{:S(2)}, u32[]{:S(2)}) %collective-permute-start.1) | collective-permute-done | bytes 86048 | tf_op jit(solution)/shard_map/ppermute | solution.py:278
  72.8 1.0 collective-permute-done.2
  73.9 1.6 %collective-permute-start.4 = (f32[168,128]{1,0:T(8,128)S(1)}, f32[168,128]{1,0:T(8,128)S(1)}, u32[]{:S(2)}, u32[]{:S(2)}) collective-permute-start(f32[168,128]{1,0:T(8,128)S(1)} %add_add_fusion.2), channel_id=1, source_target_pairs={{0,16},{1,17},{2,18},{3,19},{4,20},{5,21},{6,22},{7,23},{8,24},{9,... | collective-permute-start | bytes 258056 | tf_op jit(solution)/shard_map/ppermute | solution.py:278
  76.0 2.7 %collective-permute-start.6 = (f32[168,128]{1,0:T(8,128)S(1)}, f32[168,128]{1,0:T(8,128)S(1)}, u32[]{:S(2)}, u32[]{:S(2)}) collective-permute-start(f32[168,128]{1,0:T(8,128)S(1)} %add_add_fusion.2), channel_id=1, source_target_pairs={{0,24},{1,25},{2,26},{3,27},{4,28},{5,29},{6,30},{7,31},{8,0},{9,1... | collective-permute-start | bytes 258056 | tf_op jit(solution)/shard_map/ppermute | solution.py:278
  78.8 1.9 %collective-permute-done.4 = f32[168,128]{1,0:T(8,128)S(1)} collective-permute-done((f32[168,128]{1,0:T(8,128)S(1)}, f32[168,128]{1,0:T(8,128)S(1)}, u32[]{:S(2)}, u32[]{:S(2)}) %collective-permute-start.4) | collective-permute-done | bytes 86048 | tf_op jit(solution)/shard_map/ppermute | solution.py:278
  80.7 1.1 collective-permute-done.5
  81.8 1.3 %collective-permute-start.7 = (f32[168,128]{1,0:T(8,128)S(1)}, f32[168,128]{1,0:T(8,128)S(1)}, u32[]{:S(2)}, u32[]{:S(2)}) collective-permute-start(f32[168,128]{1,0:T(8,128)S(1)} %add_add_fusion.1), channel_id=1, source_target_pairs={{0,64},{1,65},{2,66},{3,67},{4,68},{5,69},{6,70},{7,71},{8,72},{9,... | collective-permute-start | bytes 258056 | tf_op jit(solution)/shard_map/ppermute | solution.py:278
  83.4 2.9 %collective-permute-start.9 = (f32[168,128]{1,0:T(8,128)S(1)}, f32[168,128]{1,0:T(8,128)S(1)}, u32[]{:S(2)}, u32[]{:S(2)}) collective-permute-start(f32[168,128]{1,0:T(8,128)S(1)} %add_add_fusion.1), channel_id=1, source_target_pairs={{0,96},{1,97},{2,98},{3,99},{4,100},{5,101},{6,102},{7,103},{8,104... | collective-permute-start | bytes 258056 | tf_op jit(solution)/shard_map/ppermute | solution.py:278
  86.3 6.7 %cross_kernel.1 = f32[2048,128]{1,0:T(8,128)} custom-call(s32[1,4096]{1,0:T(1,128)} %bitcast.29, bf16[4096,128]{1,0:T(8,128)(2,1)} %get-tuple-element.22.loaded), custom_call_target="tpu_custom_call" | custom-call | tf_op jit(solution)/shard_map/cross_kernel/pallas_call | solution.py:242
  93.1 6.0 %all-to-all-start.2 = ((f32[128,16,128]{2,1,0:T(8,128)}), f32[128,16,128]{2,1,0:T(8,128)S(1)}, u32[]{:S(2)}, u32[]{:S(2)}) async-start(f32[128,16,128]{2,1,0:T(8,128)} %bitcast.17), calls=%async_computation.2 | async-start | bytes 2097152 | tf_op jit(solution)/shard_map/all_to_all | solution.py:319
  99.2 1.3 %bitcast_subtract_fusion = f32[16]{0:T(128)} fusion(f32[2048]{0:T(1024)} %param.13, s32[]{:T(128)S(6)} %select_n.4, f32[2,16]{1,0:T(2,128)S(1)} %constant_dynamic-slice_fusion), kind=kLoop, calls=%fused_computation.7 | loop fusion | flops 48 | bytes 196 | tf_op jit(solution)/shard_map/sub | solution.py:332
  102.2 15.7 %all-to-all-done.2 = f32[128,16,128]{2,1,0:T(8,128)S(1)} async-done(((f32[128,16,128]{2,1,0:T(8,128)}), f32[128,16,128]{2,1,0:T(8,128)S(1)}, u32[]{:S(2)}, u32[]{:S(2)}) %all-to-all-start.2) | async-done | bytes 1048608 | tf_op jit(solution)/shard_map/all_to_all | solution.py:319
  (25 shorter events, 7.0 us)
Async XLA Ops:
  7.2 24.4 %all-to-all-start = ((f32[128,8,128]{2,1,0:T(8,128)}), f32[128,8,128]{2,1,0:T(8,128)S(1)}, u32[]{:S(2)}, u32[]{:S(2)}) async-start(f32[128,8,128]{2,1,0:T(8,128)} %bitcast.20), calls=%async_computation | async-start | bytes 1048576 | tf_op jit(solution)/shard_map/all_to_all | solution.py:285
  31.6 0.8 copy-start
  35.6 18.3 %all-to-all-start.1 = ((f32[128,8,128]{2,1,0:T(8,128)}), f32[128,8,128]{2,1,0:T(8,128)S(1)}, u32[]{:S(2)}, u32[]{:S(2)}) async-start(f32[128,8,128]{2,1,0:T(8,128)} %bitcast.21), calls=%async_computation.1 | async-start | bytes 1048576 | tf_op jit(solution)/shard_map/all_to_all | solution.py:285
  53.9 0.8 copy-start.1
  63.5 1.5 %collective-permute-start = (f32[168,128]{1,0:T(8,128)}, f32[168,128]{1,0:T(8,128)S(1)}, u32[]{:S(2)}, u32[]{:S(2)}) collective-permute-start(f32[168,128]{1,0:T(8,128)} %get-tuple-element.21), channel_id=1, source_target_pairs={{0,4},{1,5},{2,6},{3,7},{4,0},{5,1},{6,2},{7,3},{8,12},{9,13},{10,... | collective-permute-start | bytes 258056 | tf_op jit(solution)/shard_map/ppermute | solution.py:271
  65.9 7.0 %collective-permute-start.1 = (f32[168,128]{1,0:T(8,128)S(1)}, f32[168,128]{1,0:T(8,128)S(1)}, u32[]{:S(2)}, u32[]{:S(2)}) collective-permute-start(f32[168,128]{1,0:T(8,128)S(1)} %add.44), channel_id=1, source_target_pairs={{0,2},{1,3},{2,0},{3,1},{4,6},{5,7},{6,4},{7,5},{8,10},{9,11},{10,... | collective-permute-start | bytes 258056 | tf_op jit(solution)/shard_map/ppermute | solution.py:278
  67.3 6.5 %collective-permute-start.2 = (f32[168,128]{1,0:T(8,128)S(1)}, f32[168,128]{1,0:T(8,128)S(1)}, u32[]{:S(2)}, u32[]{:S(2)}) collective-permute-start(f32[168,128]{1,0:T(8,128)S(1)} %add.44), channel_id=1, source_target_pairs={{0,1},{1,2},{2,3},{3,0},{4,5},{5,6},{6,7},{7,4},{8,9},{9,10},{10,1... | collective-permute-start | bytes 258056 | tf_op jit(solution)/shard_map/ppermute | solution.py:278
  68.3 5.6 %collective-permute-start.3 = (f32[168,128]{1,0:T(8,128)S(1)}, f32[168,128]{1,0:T(8,128)S(1)}, u32[]{:S(2)}, u32[]{:S(2)}) collective-permute-start(f32[168,128]{1,0:T(8,128)S(1)} %add.44), channel_id=1, source_target_pairs={{0,3},{1,0},{2,1},{3,2},{4,7},{5,4},{6,5},{7,6},{8,11},{9,8},{10,9... | collective-permute-start | bytes 258056 | tf_op jit(solution)/shard_map/ppermute | solution.py:278
  73.9 6.8 %collective-permute-start.4 = (f32[168,128]{1,0:T(8,128)S(1)}, f32[168,128]{1,0:T(8,128)S(1)}, u32[]{:S(2)}, u32[]{:S(2)}) collective-permute-start(f32[168,128]{1,0:T(8,128)S(1)} %add_add_fusion.2), channel_id=1, source_target_pairs={{0,16},{1,17},{2,18},{3,19},{4,20},{5,21},{6,22},{7,23},{8,24},{9,... | collective-permute-start | bytes 258056 | tf_op jit(solution)/shard_map/ppermute | solution.py:278
  75.5 6.3 %collective-permute-start.5 = (f32[168,128]{1,0:T(8,128)S(1)}, f32[168,128]{1,0:T(8,128)S(1)}, u32[]{:S(2)}, u32[]{:S(2)}) collective-permute-start(f32[168,128]{1,0:T(8,128)S(1)} %add_add_fusion.2), channel_id=1, source_target_pairs={{0,8},{1,9},{2,10},{3,11},{4,12},{5,13},{6,14},{7,15},{8,16},{9,17... | collective-permute-start | bytes 258056 | tf_op jit(solution)/shard_map/ppermute | solution.py:278
  76.0 5.7 %collective-permute-start.6 = (f32[168,128]{1,0:T(8,128)S(1)}, f32[168,128]{1,0:T(8,128)S(1)}, u32[]{:S(2)}, u32[]{:S(2)}) collective-permute-start(f32[168,128]{1,0:T(8,128)S(1)} %add_add_fusion.2), channel_id=1, source_target_pairs={{0,24},{1,25},{2,26},{3,27},{4,28},{5,29},{6,30},{7,31},{8,0},{9,1... | collective-permute-start | bytes 258056 | tf_op jit(solution)/shard_map/ppermute | solution.py:278
  81.8 17.2 %collective-permute-start.7 = (f32[168,128]{1,0:T(8,128)S(1)}, f32[168,128]{1,0:T(8,128)S(1)}, u32[]{:S(2)}, u32[]{:S(2)}) collective-permute-start(f32[168,128]{1,0:T(8,128)S(1)} %add_add_fusion.1), channel_id=1, source_target_pairs={{0,64},{1,65},{2,66},{3,67},{4,68},{5,69},{6,70},{7,71},{8,72},{9,... | collective-permute-start | bytes 258056 | tf_op jit(solution)/shard_map/ppermute | solution.py:278
  83.1 16.0 %collective-permute-start.8 = (f32[168,128]{1,0:T(8,128)S(1)}, f32[168,128]{1,0:T(8,128)S(1)}, u32[]{:S(2)}, u32[]{:S(2)}) collective-permute-start(f32[168,128]{1,0:T(8,128)S(1)} %add_add_fusion.1), channel_id=1, source_target_pairs={{0,32},{1,33},{2,34},{3,35},{4,36},{5,37},{6,38},{7,39},{8,40},{9,... | collective-permute-start | bytes 258056 | tf_op jit(solution)/shard_map/ppermute | solution.py:278
  83.4 15.6 %collective-permute-start.9 = (f32[168,128]{1,0:T(8,128)S(1)}, f32[168,128]{1,0:T(8,128)S(1)}, u32[]{:S(2)}, u32[]{:S(2)}) collective-permute-start(f32[168,128]{1,0:T(8,128)S(1)} %add_add_fusion.1), channel_id=1, source_target_pairs={{0,96},{1,97},{2,98},{3,99},{4,100},{5,101},{6,102},{7,103},{8,104... | collective-permute-start | bytes 258056 | tf_op jit(solution)/shard_map/ppermute | solution.py:278
  93.1 24.8 %all-to-all-start.2 = ((f32[128,16,128]{2,1,0:T(8,128)}), f32[128,16,128]{2,1,0:T(8,128)S(1)}, u32[]{:S(2)}, u32[]{:S(2)}) async-start(f32[128,16,128]{2,1,0:T(8,128)} %bitcast.17), calls=%async_computation.2 | async-start | bytes 2097152 | tf_op jit(solution)/shard_map/all_to_all | solution.py:319

commit v2 on v1

--- a/solution.py
+++ b/solution.py
@@ -1,3 +1,4 @@
+import functools
 import math
 
 import jax
@@ -5,11 +6,14 @@
 from jax import lax
 from jax.experimental import pallas as pl
 from jax.experimental.pallas import tpu as pltpu
+from jax.sharding import Mesh
 from jax.sharding import PartitionSpec as P
+
 
 STRATA = 512
 CENTERS_DEV = 16
-AXES = ("tm", "rows")
+AXES = ("z", "y", "core", "x")
+CHIPS = ("z", "y", "x")
 BLOCK = 512
 LANES = 128
 F32 = jnp.float32
@@ -89,7 +93,7 @@
     return pl.ds(start, count, stride=8)
 
 
-def weigh_kernel(counts, strata, centers, covars, beta, frailty, w_out, wx_out, send):
+def weigh_kernel(counts, strata, centers, beta, frailty, covars, w_out, send):
     records = covars.shape[0]
     betas = stack(split3(beta[...]), 8)
     table = table_rows(frailty[...])
@@ -105,10 +109,10 @@
         weight = jnp.where(live, jnp.exp(eta), 0.0)
         w_out[:, span] = weight
         weighted = (columns(split3(weight)) * rows.astype(F32)).astype(BF16)
-        wx_out[span, :] = weighted
         total_one = total_one + mxu(one_hot(ids, STRATA), weighted)
         total_zero = total_zero + add_up(weight, ids >> 7, one_hot(ids & 127, LANES), 8)
-    devices = send.shape[0] // 8
+    devices = send.shape[0]
+    send = send.reshape(devices * 8, LANES)
     for place in range(4):
         send[strided(place, devices), :] = jnp.broadcast_to(
             total_zero[place : place + 1], (devices, LANES)
@@ -116,13 +120,14 @@
         send[strided(4 + place, devices), :] = total_one[place * LANES : (place + 1) * LANES]
 
 
-def suffix_kernel(strata, w_in, wx_in, zero_out, one_out):
-    records = wx_in.shape[0]
+def suffix_kernel(strata, w_in, covars, zero_out, one_out):
+    records = covars.shape[0]
     carry_zero = jnp.zeros((8, LANES), F32)
     carry_one = jnp.zeros((STRATA, LANES), F32)
     for start in reversed(range(0, records, BLOCK)):
         span = pl.ds(start, BLOCK)
-        ids, weight, weighted = strata[:, span], w_in[:, span], wx_in[span, :]
+        ids, weight = strata[:, span], w_in[:, span]
+        weighted = (columns(split3(weight)) * covars[span, :].astype(F32)).astype(BF16)
         id_column = id_columns(ids)
         shared = same_and_later(ids, id_column)
         lower_hot = one_hot(ids & 127, LANES)
@@ -138,7 +143,9 @@
 
 def hazard_kernel(counts, mine, strata, events, zero_in, received, q_out, send, later):
     records = strata.shape[1]
-    devices = received.shape[0] // 8
+    devices = received.shape[0]
+    received = received.reshape(devices * 8, LANES)
+    send = send.reshape(devices * 8, LANES)
     running = jnp.zeros((8, LANES), F32)
     for device in reversed(range(devices)):
         slab = pl.ds(device * 8, 8)
@@ -176,11 +183,12 @@
 
 
 def moments_kernel(
-    counts, mine, strata, centers, events, w_in, q_in, hazard_in, covars, one_in, received,
-    loaded_out, pack,
+    counts, mine, strata, centers, events, w_in, q_in, hazard_in, received, covars, one_in,
+    loaded_out, pack, low_out,
 ):
     records, width = covars.shape
-    devices = received.shape[0] // 8
+    devices = received.shape[0]
+    received = received.reshape(devices * 8, LANES)
     before = (iota((devices * 8, LANES), 0) >> 3) < mine[0]
     earlier = jnp.where(before, received[...], 0.0).reshape(devices, 8, LANES).sum(axis=0)
     table = table_rows(earlier)
@@ -188,10 +196,10 @@
     high = later.astype(BF16)
     low = (later - high.astype(F32)).astype(BF16)
     later = jnp.concatenate([high, low], axis=1)
-    sixteen = iota((16, 2 * LANES), 0)
-    left = iota((16, 2 * LANES), 1) < LANES
+    sixteen = iota((16, 3 * LANES), 0)
+    group = iota((16, 3 * LANES), 1) >> 7
     spread = jnp.where(
-        (left & (sixteen < 3)) | (~left & (sixteen >= 3) & (sixteen < 6)), 1.0, 0.0
+        (sixteen < 8) & (group == jnp.where(sixteen < 3, 0, jnp.where(sixteen < 6, 1, 2))), 1.0, 0.0
     ).astype(BF16)
     groups = 16
     pairs = jnp.zeros((4 * groups, LANES), F32)
@@ -206,13 +214,14 @@
         live = iota((1, BLOCK), 1) + start < counts[0]
         happened = jnp.where(live & (events[:, span] > 0), 1.0, 0.0)
         parts = split3(exposure)
-        both = mxu(stack([*parts, *split3(increment)], 16), spread, TN)
+        top = ids & ~255
+        both = mxu(stack([*parts, *split3(increment), top.astype(F32), (ids - top).astype(F32)], 16), spread, TN)
         loaded = (both[:, :LANES] * rows.astype(F32)).astype(BF16)
         loaded_out[span, :] = loaded
-        outside = mxu(members(id_columns(ids)), later)
-        mean = (one_in[span, :] + outside[:, :LANES] + outside[:, LANES:]) * both[:, LANES:]
+        outside = mxu(members(jnp.concatenate([both[:, 2 * LANES :]] * 4, axis=1)), later)
+        mean = (one_in[span, :] + outside[:, :LANES] + outside[:, LANES:]) * both[:, LANES : 2 * LANES]
         mean_low = mean.astype(BF16)
-        curvature = curvature + mxu(rows, loaded, TN) - mxu(mean_low, mean_low, TN)
+        low_out[span, :] = mean_low
         flags = mxu(stack([happened], 8), rows)
         gradient = gradient + flags[:1] - jnp.sum(mean, axis=0, keepdims=True)
         at = iota((groups, BLOCK), 0)
@@ -220,6 +229,7 @@
         pairs = pairs + mxu(
             jnp.concatenate(chosen, axis=0).astype(BF16), one_hot(owners & 127, LANES), NT
         )
+    curvature = mxu(covars[...], loaded_out[...], TN) - mxu(low_out[...], low_out[...], TN)
     exposed = pairs[:groups] + pairs[groups : 2 * groups] + pairs[2 * groups : 3 * groups]
     pack[0:width, :] = curvature
     pack[width : width + 8, :] = jnp.broadcast_to(gradient, (8, width))
@@ -227,33 +237,74 @@
     pack[width + 24 : width + 40, :] = exposed
 
 
-def cross_kernel(centers, loaded, out):
-    tile = 256
-    for start in range(0, out.shape[0], tile):
-        out[pl.ds(start, tile), :] = mxu(one_hot(centers[...] - start, tile), loaded[...])
-
-
-def call(kernel, out_shape, scratch=(), scalars=0, **kwargs):
+def cross_kernel(centers, loaded, core_zero, core_one):
+    records, width = loaded.shape
+    groups = 8
+    ids = centers[...]
+    within = ids & 255
+    upper = jnp.concatenate(
+        [columns([(ids[:, at : at + BLOCK] >> 8).astype(F32)]) for at in range(0, records, BLOCK)],
+        axis=0,
+    ).astype(BF16)
+    rows = loaded[...]
+    chosen = jnp.concatenate(
+        [jnp.where(upper == group, rows, jnp.zeros_like(rows)) for group in range(groups)], axis=1
+    )
+    place = ((within >> 6) & 1) * LANES + (within >> 7) * 64 + (within & 63)
+    sums = mxu(one_hot(place, 2 * LANES), chosen)
+    for group in range(groups):
+        lanes = pl.ds(group * width, width)
+        part = sums[:, group * width : (group + 1) * width]
+        core_zero[pl.ds(group * LANES, LANES), :] = part[:LANES]
+        core_one[pl.ds(group * LANES, LANES), :] = part[LANES:]
+
+
+def last_kernel(
+    load, devices, mine, first, second, third, fourth, shares, frailty,
+    info, score, center_score, center_info, center_cross,
+):
+    width = info.shape[0]
+    pack = (first[...] + third[...]) + (second[...] + fourth[...])
+    total = load * CENTERS_DEV * devices
+    root = math.sqrt(load)
+    info[...] = pack[:width] / total
+    score[...] = pack[width : width + 1] / math.sqrt(total)
+    hit = iota((16, LANES), 0) == mine[0] >> 3
+    turn = (LANES - (mine[0] & 7) * CENTERS_DEV) & (LANES - 1)
+
+    def own(table):
+        row = jnp.sum(jnp.where(hit, table, 0.0), axis=0, keepdims=True)
+        return pltpu.roll(jnp.broadcast_to(row, (8, LANES)), turn, 1)[:1]
+
+    own_score = own(pack[width + 8 : width + 24]) / root - 0.5 * own(frailty[...])
+    own_info = own(pack[width + 24 :]) / load + 0.5
+    center_score[...] = own_score[:, :CENTERS_DEV]
+    center_info[...] = own_info[:, :CENTERS_DEV]
+    center_cross[...] = jnp.sum(shares[...], axis=0) / root
+
+
+def call(kernel, out_shape, scratch=(), scalars=0, near=True):
     def run(*args):
-        specs = [
-            pl.BlockSpec(memory_space=pltpu.SMEM if place < scalars else pltpu.VMEM)
-            for place in range(len(args))
-        ]
+        arrays = len(args) - scalars
+        spaces = [pltpu.SMEM] * scalars + [pltpu.VMEM] * arrays
+        place = pltpu.VMEM if near else pltpu.HBM
         return pl.pallas_call(
             kernel,
             out_shape=out_shape,
-            in_specs=specs,
+            in_specs=[pl.BlockSpec(memory_space=space) for space in spaces],
             out_specs=jax.tree.map(lambda _: pl.BlockSpec(memory_space=pltpu.VMEM), out_shape),
             scratch_shapes=list(scratch),
-            name=kernel.__name__,
-            **kwargs,
-        )(*args)
+            compiler_params=pltpu.CompilerParams(vmem_limit_bytes=12 * 2**20),
+        )(
+            *args[:scalars],
+            *(pltpu.with_memory_space_constraint(arg, place) for arg in args[scalars:]),
+        )
 
     return run
 
 
 def shaped(*shape, dtype=F32):
-    return jax.ShapeDtypeStruct(shape, dtype)
+    return pltpu.VMEM(shape, dtype)
 
 
 def place_of(z, y, c, x):
@@ -267,40 +318,48 @@
     return [(place_of(*at), place_of(*step(*at))) for at in grid]
 
 
-def sum_everywhere(value):
-    value = value + lax.ppermute(value, AXES, moves(lambda z, y, c, x: (z, y, 1 - c, x)))
-    rings = (
-        lambda k: lambda z, y, c, x: (z, y, c, (x + k) % 4),
-        lambda k: lambda z, y, c, x: (z, (y + k) % 4, c, x),
-        lambda k: lambda z, y, c, x: ((z + k) % 4, y, c, x),
-    )
-    for ring in rings:
-        others = [lax.ppermute(value, AXES, moves(ring(k))) for k in (1, 2, 3)]
-        value = (value + others[1]) + (others[0] + others[2])
-    return value
-
-
-def exchange(value):
-    devices = value.shape[0] // 8
-    out = lax.all_to_all(value.reshape(devices, 8, LANES), AXES, 0, 0, tiled=True)
-    return out.reshape(devices * 8, LANES)
+def gather_ring(value, name):
+    axis = "zyx".index(name)
+
+    def ahead(k):
+        def step(z, y, c, x):
+            at = [z, y, x]
+            at[axis] = (at[axis] + k) % 4
+            return at[0], at[1], c, at[2]
+
+        return step
+
+    return [value] + [lax.ppermute(value, AXES, moves(ahead(k))) for k in (1, 2, 3)]
+
+
+def sum_ring(value, name):
+    here, one, two, three = gather_ring(value, name)
+    return (here + two) + (one + three)
+
+
+def other_core(value):
+    return lax.ppermute(value, AXES, moves(lambda z, y, c, x: (z, y, 1 - c, x)))
+
+
+def exchange(value, axes=AXES):
+    return lax.all_to_all(value, axes, 0, 0, tiled=True)
 
 
 def body(covars, strata, centers, events, counts, beta, frailty):
     records, width = covars.shape
-    devices = lax.axis_size("tm") * lax.axis_size("rows")
+    devices = math.prod(lax.axis_size(axis) for axis in AXES)
     center_total = CENTERS_DEV * devices
     mine = lax.axis_index(AXES)
     me = mine.reshape(1).astype(jnp.int32)
     strata, centers, events = (part.reshape(1, records) for part in (strata, centers, events))
-    slabs = shaped(devices * 8, LANES)
+    slabs = shaped(devices, 8, LANES)
     line = shaped(1, records)
-    weights, weighted, totals = call(
-        weigh_kernel, (line, shaped(records, width, dtype=BF16), slabs), scalars=1
-    )(counts, strata, centers, covars, beta.reshape(1, width), frailty.reshape(-1, LANES))
+    weights, totals = call(weigh_kernel, (line, slabs), scalars=1, near=False)(
+        counts, strata, centers, beta.reshape(1, width), frailty.reshape(-1, LANES), covars
+    )
     received = exchange(totals)
     suffix_zero, suffix_one = call(suffix_kernel, (line, shaped(records, width)))(
-        strata, weights, weighted
+        strata, weights, covars
     )
     increments, send = call(
         hazard_kernel, (line, slabs), scratch=[pltpu.VMEM((devices * 8, LANES), F32)], scalars=2
@@ -309,33 +368,49 @@
     local_hazard = call(prefix_kernel, line)(strata, increments)
     loaded, pack = call(
         moments_kernel,
-        (shaped(records, width, dtype=BF16), shaped(width + 40, LANES)),
+        (pltpu.HBM((records, width), BF16), shaped(width + 40, LANES)),
+        scratch=[pltpu.VMEM((records, width), BF16)],
         scalars=2,
     )(
-        counts, me, strata, centers, events, weights, increments, local_hazard, covars,
-        suffix_one, arrived,
-    )
-    cross = call(cross_kernel, shaped(center_total, width))(centers, loaded)
-    shares = lax.all_to_all(
-        cross.reshape(devices, CENTERS_DEV, width), AXES, 0, 0, tiled=True
-    )
-    pack = sum_everywhere(pack)
-    total = records * devices
-    info = pack[:width] / total
-    score = pack[width] / math.sqrt(total)
-    load = records // CENTERS_DEV
-    root = math.sqrt(load)
-    pairs = pack[width + 8 :].reshape(2, center_total)
-    first = mine * CENTERS_DEV
-    pairs = lax.dynamic_slice_in_dim(pairs, first, CENTERS_DEV, axis=1)
-    frailty_mine = lax.dynamic_slice_in_dim(frailty, first, CENTERS_DEV)
-    center_score = pairs[0] / root - 0.5 * frailty_mine
-    center_info = pairs[1] / load + 0.5
-    center_cross = jnp.sum(shares, axis=0) / root
-    return (score, info, center_score, center_info, center_cross)
+        counts, me, strata, centers, events, weights, increments, local_hazard, arrived,
+        covars, suffix_one,
+    )
+    swapped = other_core(pack)
+    half = shaped(center_total // 2, width)
+    core_zero, core_one = call(cross_kernel, (half, half), near=False)(centers, loaded)
+    pack = sum_ring(pack + swapped, "x")
+    is_one = lax.axis_index("core") == 1
+    keep = jnp.where(is_one, core_one, core_zero)
+    give = jnp.where(is_one, core_zero, core_one)
+    cross = keep + other_core(give)
+    shares = exchange(cross.reshape(devices // 2, CENTERS_DEV, width), CHIPS)
+    pack = sum_ring(pack, "y")
+    parts = gather_ring(pack, "z")
+    last = call(
+        functools.partial(last_kernel, records // CENTERS_DEV, devices),
+        (
+            jax.ShapeDtypeStruct((width, width), F32),
+            jax.ShapeDtypeStruct((1, width), F32),
+            jax.ShapeDtypeStruct((1, CENTERS_DEV), F32),
+            jax.ShapeDtypeStruct((1, CENTERS_DEV), F32),
+            jax.ShapeDtypeStruct((CENTERS_DEV, width), F32),
+        ),
+        scalars=1,
+    )
+    info, score, center_score, center_info, center_cross = last(
+        me, *parts, shares, frailty.reshape(-1, LANES)
+    )
+    return (
+        score.reshape(width),
+        info,
+        center_score.reshape(CENTERS_DEV),
+        center_info.reshape(CENTERS_DEV),
+        center_cross,
+    )
 
 
 def solution(mesh):
+    mesh = Mesh(mesh.devices.reshape(4, 4, 2, 4), AXES)
     in_specs = (
         P(AXES, None),
         P(AXES),

time: 120 us -> 99.7 us (0.83)
  Pallas kernels: 36.4 us -> 27.2 us
  waiting for transfers between devices: 37.8 us -> 31.3 us
  other arithmetic: 4.65 us -> 1 us
    all_to_all x3, waiting for transfers between devices: 30.1 us -> 17.1 us  [exchange(): return lax.all_to_all(value, axes, 0, 0, tiled=True)]
    pallas_call x6 -> x7, Pallas kernels: 36.4 us -> 27.2 us  [run(): pl.pallas_call(kernel, out_shape=out_shape, in_specs=[pl.BlockSpec(memory...]
    ppermute x10 -> x11, waiting for transfers between devices: 7.69 us -> 14.2 us  [the longest x9 12.7 us: gather_ring(): lax.ppermute(value, AXES, moves(ahead(k)))]
    div x3 -> x0, other arithmetic: 1.75 us -> none  [the longest x1 0.63 us: body(): info = pack[:width] / total]
    sub x1 -> x0, other arithmetic: 1.27 us -> none  [body(): center_score = pairs[0] / root - 0.5 * frailty_mine]
    ppermute x10 -> x11, starting transfers between devices: 14.2 us -> 13.9 us  [the longest x9 13.3 us: gather_ring(): lax.ppermute(value, AXES, moves(ahead(k)))]
  transfers between devices with their start and end apart: 13 -> 14, of which waited for: 8 -> 9; matrix products, arithmetic and copies ran while one was open for 3% -> 1% of each run, Pallas kernels for 16% -> 8%
where the time goes in v2:
time: 99.7 us; the launch traced here: 99.2 us
  starting transfers between devices  37.3 us (37%)
  waiting for transfers between devices  31.3 us (31%)
  Pallas kernels  27.2 us (27%)
  between operations  1.54 us (2%)
  other arithmetic  1 us (1%)
    pallas_call x7, Pallas kernels, run(): pl.pallas_call(kernel, out_shape=out_shape, in_specs=[pl.BlockSpec(memory...  27.2 us
    all_to_all x3, starting transfers between devices, exchange(): return lax.all_to_all(value, axes, 0, 0, tiled=True)  23.4 us
    all_to_all x3, waiting for transfers between devices, exchange(): return lax.all_to_all(value, axes, 0, 0, tiled=True)  17.1 us
    ppermute x9, starting transfers between devices, gather_ring(): lax.ppermute(value, AXES, moves(ahead(k)))  13.3 us
    ppermute x9, waiting for transfers between devices, gather_ring(): lax.ppermute(value, AXES, moves(ahead(k)))  12.7 us
  transfers between devices with their start and end apart: 14, of which 9 were waited for; matrix products, arithmetic and copies ran while one was open for 1% of the time, Pallas kernels for 8%

profile of v2, /device:TPU:0, one launch (start us, length us, event | category | flops | bytes accessed | tf_op | source)
XLA Modules:
  0.0 99.2 jit_solution(2474479416006539357)
XLA Ops:
  1.4 6.0 %shard_map.110 = (f32[1,4096]{1,0:T(1,128)S(1)}, f32[128,8,128]{2,1,0:T(8,128)}) custom-call(s32[1]{0:T(128)S(6)} %copy.12.counts, s32[1,4096]{1,0:T(1,128)} %bitcast.10, s32[1,4096]{1,0:T(1,128)} %bitcast.15, f32[1,128]{1,0:T(1,128)} %bitcast.22, f32[16,128]{1,0:T(8,128)} %bitcast.20, bf16[4096,128]{1,0:T(8,128)(2,1)} %covars.5), custom_call_target="tpu_custom_call" | custom-call | tf_op jit(solution)/shard_map/pallas_call | solution.py:291
  7.4 11.7 %all-to-all-start = ((f32[128,8,128]{2,1,0:T(8,128)}), f32[128,8,128]{2,1,0:T(8,128)}, u32[]{:S(2)}, u32[]{:S(2)}) async-start(f32[128,8,128]{2,1,0:T(8,128)} %get-tuple-element.22), calls=%async_computation | async-start | bytes 1048576 | tf_op jit(solution)/shard_map/all_to_all | solution.py:345
  19.1 6.3 %shard_map.111 = (f32[1,4096]{1,0:T(1,128)S(1)}, f32[4096,128]{1,0:T(8,128)S(1)}) custom-call(s32[1,4096]{1,0:T(1,128)S(1)} %bitcast.11, f32[1,4096]{1,0:T(1,128)S(1)} %get-tuple-element.20.w_in, bf16[4096,128]{1,0:T(8,128)(2,1)S(1)} %copy-done), custom_call_target="tpu_custom_call" | custom-call | tf_op jit(solution)/shard_map/pallas_call | solution.py:291
  25.4 6.4 %all-to-all-done.received = f32[128,8,128]{2,1,0:T(8,128)} async-done(((f32[128,8,128]{2,1,0:T(8,128)}), f32[128,8,128]{2,1,0:T(8,128)}, u32[]{:S(2)}, u32[]{:S(2)}) %all-to-all-start) | async-done | bytes 524320 | tf_op jit(solution)/shard_map/all_to_all | solution.py:345
  31.9 2.3 %shard_map.112 = (f32[1,4096]{1,0:T(1,128)S(1)}, f32[128,8,128]{2,1,0:T(8,128)S(1)}) custom-call(s32[1]{0:T(128)S(6)} %copy.12.counts, s32[1]{0:T(128)} %bitcast.mine, s32[1,4096]{1,0:T(1,128)S(1)} %bitcast.12, s32[1,4096]{1,0:T(1,128)S(1)} %bitcast.18, f32[1,4096]{1,0:T(1,128)S(1)} %get-tuple-element.21.zero_in, f32[128,8,128]{2,1,0:T(8,128)} %all-to-all-done.received), custom_call_target="tpu_custom_call" | custom-call | tf_op jit(solution)/shard_map/pallas_call | solution.py:291
  35.0 5.9 %all-to-all-start.1 = ((f32[128,8,128]{2,1,0:T(8,128)}), f32[128,8,128]{2,1,0:T(8,128)}, u32[]{:S(2)}, u32[]{:S(2)}) async-start(f32[128,8,128]{2,1,0:T(8,128)} %copy-done.1), calls=%async_computation.1 | async-start | bytes 1048576 | tf_op jit(solution)/shard_map/all_to_all | solution.py:345
  41.0 1.9 %shard_map.113.hazard_in = f32[1,4096]{1,0:T(1,128)S(1)} custom-call(s32[1,4096]{1,0:T(1,128)S(1)} %bitcast.13, f32[1,4096]{1,0:T(1,128)S(1)} %get-tuple-element.23.q_in), custom_call_target="tpu_custom_call" | custom-call | tf_op jit(solution)/shard_map/pallas_call | solution.py:291
  42.9 10.7 %all-to-all-done.1.received = f32[128,8,128]{2,1,0:T(8,128)} async-done(((f32[128,8,128]{2,1,0:T(8,128)}), f32[128,8,128]{2,1,0:T(8,128)}, u32[]{:S(2)}, u32[]{:S(2)}) %all-to-all-start.1) | async-done | bytes 524320 | tf_op jit(solution)/shard_map/all_to_all | solution.py:345
  53.6 6.0 %shard_map.114 = (bf16[4096,128]{1,0:T(8,128)(2,1)}, f32[168,128]{1,0:T(8,128)S(1)}) custom-call(s32[1]{0:T(128)S(6)} %copy.12.counts, s32[1]{0:T(128)} %bitcast.mine, s32[1,4096]{1,0:T(1,128)S(1)} %bitcast.14, s32[1,4096]{1,0:T(1,128)S(1)} %bitcast.17, s32[1,4096]{1,0:T(1,128)S(1)} %bitcast.19, f32[1,4096]{1,0:T(1,128)S(1)} %get-tuple-element.20.w_in, ...), custom_call_target="tpu_custom_call" | custom-call | tf_op jit(solution)/shard_map/pallas_call | solution.py:291
  59.6 3.9 %shard_map.115 = (f32[1024,128]{1,0:T(8,128)S(1)}, f32[1024,128]{1,0:T(8,128)S(1)}) custom-call(s32[1,4096]{1,0:T(1,128)} %bitcast.16, bf16[4096,128]{1,0:T(8,128)(2,1)} %get-tuple-element.27.loaded), custom_call_target="tpu_custom_call" | custom-call | tf_op jit(solution)/shard_map/pallas_call | solution.py:291
  64.2 1.5 %collective-permute-done = f32[168,128]{1,0:T(8,128)S(1)} collective-permute-done((f32[168,128]{1,0:T(8,128)S(1)}, f32[168,128]{1,0:T(8,128)S(1)}, u32[]{:S(2)}, u32[]{:S(2)}) %collective-permute-start) | collective-permute-done | bytes 86048 | tf_op jit(solution)/shard_map/ppermute | solution.py:341
  65.7 1.5 %collective-permute-start.3 = (f32[168,128]{1,0:T(8,128)S(1)}, f32[168,128]{1,0:T(8,128)S(1)}, u32[]{:S(2)}, u32[]{:S(2)}) collective-permute-start(f32[168,128]{1,0:T(8,128)S(1)} %add.36), channel_id=1, source_target_pairs={{0,3},{1,0},{2,1},{3,2},{4,7},{5,4},{6,5},{7,6},{8,11},{9,8},{10,9... | collective-permute-start | bytes 258056 | tf_op jit(solution)/shard_map/ppermute | solution.py:332
  67.8 1.4 %collective-permute-start.1 = (f32[168,128]{1,0:T(8,128)S(1)}, f32[168,128]{1,0:T(8,128)S(1)}, u32[]{:S(2)}, u32[]{:S(2)}) collective-permute-start(f32[168,128]{1,0:T(8,128)S(1)} %add.36), channel_id=1, source_target_pairs={{0,2},{1,3},{2,0},{3,1},{4,6},{5,7},{6,4},{7,5},{8,10},{9,11},{10,... | collective-permute-start | bytes 258056 | tf_op jit(solution)/shard_map/ppermute | solution.py:332
  70.1 5.8 %all-to-all-start.2 = ((f32[64,16,128]{2,1,0:T(8,128)}), f32[64,16,128]{2,1,0:T(8,128)S(1)}, u32[]{:S(2)}, u32[]{:S(2)}) async-start(f32[64,16,128]{2,1,0:T(8,128)} %bitcast.6), calls=%async_computation.2 | async-start | bytes 1048576 | tf_op jit(solution)/shard_map/all_to_all | solution.py:345
  75.9 2.9 %collective-permute-start.6 = (f32[168,128]{1,0:T(8,128)S(1)}, f32[168,128]{1,0:T(8,128)S(1)}, u32[]{:S(2)}, u32[]{:S(2)}) collective-permute-start(f32[168,128]{1,0:T(8,128)S(1)} %add_add_fusion.1), channel_id=1, source_target_pairs={{0,24},{1,25},{2,26},{3,27},{4,28},{5,29},{6,30},{7,31},{8,0},{9,1... | collective-permute-start | bytes 258056 | tf_op jit(solution)/shard_map/ppermute | solution.py:332
  78.8 2.3 %collective-permute-start.4 = (f32[168,128]{1,0:T(8,128)S(1)}, f32[168,128]{1,0:T(8,128)S(1)}, u32[]{:S(2)}, u32[]{:S(2)}) collective-permute-start(f32[168,128]{1,0:T(8,128)S(1)} %add_add_fusion.1), channel_id=1, source_target_pairs={{0,16},{1,17},{2,18},{3,19},{4,20},{5,21},{6,22},{7,23},{8,24},{9,... | collective-permute-start | bytes 258056 | tf_op jit(solution)/shard_map/ppermute | solution.py:332
  81.1 4.3 %collective-permute-done.6 = f32[168,128]{1,0:T(8,128)S(1)} collective-permute-done((f32[168,128]{1,0:T(8,128)S(1)}, f32[168,128]{1,0:T(8,128)S(1)}, u32[]{:S(2)}, u32[]{:S(2)}) %collective-permute-start.6) | collective-permute-done | bytes 86048 | tf_op jit(solution)/shard_map/ppermute | solution.py:332
  85.4 2.1 %collective-permute-done.5 = f32[168,128]{1,0:T(8,128)S(1)} collective-permute-done((f32[168,128]{1,0:T(8,128)S(1)}, f32[168,128]{1,0:T(8,128)S(1)}, u32[]{:S(2)}, u32[]{:S(2)}) %collective-permute-start.5) | collective-permute-done | bytes 86048 | tf_op jit(solution)/shard_map/ppermute | solution.py:332
  87.5 1.0 collective-permute-done.4
  88.5 3.0 %collective-permute-start.9 = (f32[168,128]{1,0:T(8,128)S(1)}, f32[168,128]{1,0:T(8,128)S(1)}, u32[]{:S(2)}, u32[]{:S(2)}) collective-permute-start(f32[168,128]{1,0:T(8,128)S(1)} %add_add_fusion.first), channel_id=1, source_target_pairs={{0,96},{1,97},{2,98},{3,99},{4,100},{5,101},{6,102},{7,103},{8,104... | collective-permute-start | bytes 258056 | tf_op jit(solution)/shard_map/ppermute | solution.py:332
  92.2 1.0 collective-permute-start.7
  93.1 1.7 %collective-permute-done.9.fourth = f32[168,128]{1,0:T(8,128)S(1)} collective-permute-done((f32[168,128]{1,0:T(8,128)S(1)}, f32[168,128]{1,0:T(8,128)S(1)}, u32[]{:S(2)}, u32[]{:S(2)}) %collective-permute-start.9) | collective-permute-done | bytes 86048 | tf_op jit(solution)/shard_map/ppermute | solution.py:332
  94.9 2.7 %collective-permute-done.8.third = f32[168,128]{1,0:T(8,128)S(1)} collective-permute-done((f32[168,128]{1,0:T(8,128)S(1)}, f32[168,128]{1,0:T(8,128)S(1)}, u32[]{:S(2)}, u32[]{:S(2)}) %collective-permute-start.8) | collective-permute-done | bytes 86048 | tf_op jit(solution)/shard_map/ppermute | solution.py:332
  97.5 0.9 collective-permute-done.7.second
  (28 shorter events, 4.3 us)
Async XLA Ops:
  0.6 18.4 %copy-start = (bf16[4096,128]{1,0:T(8,128)(2,1)S(1)}, bf16[4096,128]{1,0:T(8,128)(2,1)}, u32[]{:S(2)}) copy-start(bf16[4096,128]{1,0:T(8,128)(2,1)} %covars.5) | copy-start | bytes 3145732
  0.6 18.4 %copy-start.2 = (s32[4096]{0:T(1024)S(1)}, s32[4096]{0:T(1024)}, u32[]{:S(2)}) copy-start(s32[4096]{0:T(1024)} %param.8) | copy-start | bytes 49156
  0.7 31.2 %copy-start.4 = (s32[4096]{0:T(1024)S(1)}, s32[4096]{0:T(1024)}, u32[]{:S(2)}) copy-start(s32[4096]{0:T(1024)} %param.10) | copy-start | bytes 49156
  7.4 46.2 %copy-start.3 = (s32[4096]{0:T(1024)S(1)}, s32[4096]{0:T(1024)}, u32[]{:S(2)}) copy-start(s32[4096]{0:T(1024)} %param.9) | copy-start | bytes 49156
  7.4 24.5 %all-to-all-start = ((f32[128,8,128]{2,1,0:T(8,128)}), f32[128,8,128]{2,1,0:T(8,128)}, u32[]{:S(2)}, u32[]{:S(2)}) async-start(f32[128,8,128]{2,1,0:T(8,128)} %get-tuple-element.22), calls=%async_computation | async-start | bytes 1048576 | tf_op jit(solution)/shard_map/all_to_all | solution.py:345
  34.2 0.8 copy-start.1
  35.0 18.5 %all-to-all-start.1 = ((f32[128,8,128]{2,1,0:T(8,128)}), f32[128,8,128]{2,1,0:T(8,128)}, u32[]{:S(2)}, u32[]{:S(2)}) async-start(f32[128,8,128]{2,1,0:T(8,128)} %copy-done.1), calls=%async_computation.1 | async-start | bytes 1048576 | tf_op jit(solution)/shard_map/all_to_all | solution.py:345
  63.6 5.6 %collective-permute-start.10 = (f32[1024,128]{1,0:T(8,128)S(1)}, f32[1024,128]{1,0:T(8,128)S(1)}, u32[]{:S(2)}, u32[]{:S(2)}) collective-permute-start(f32[1024,128]{1,0:T(8,128)S(1)} %broadcast_select_fusion), channel_id=1, source_target_pairs={{0,4},{1,5},{2,6},{3,7},{4,0},{5,1},{6,2},{7,3},{8,12},{9,13},{10,... | collective-permute-start | bytes 1572872 | tf_op jit(solution)/shard_map/ppermute | solution.py:341
  63.8 34.7 %copy-start.5 = (f32[2048]{0:T(1024)S(1)}, f32[2048]{0:T(1024)}, u32[]{:S(2)}) copy-start(f32[2048]{0:T(1024)} %param.13) | copy-start | bytes 24580
  63.8 1.9 %collective-permute-start = (f32[168,128]{1,0:T(8,128)S(1)}, f32[168,128]{1,0:T(8,128)S(1)}, u32[]{:S(2)}, u32[]{:S(2)}) collective-permute-start(f32[168,128]{1,0:T(8,128)S(1)} %get-tuple-element.26), channel_id=1, source_target_pairs={{0,4},{1,5},{2,6},{3,7},{4,0},{5,1},{6,2},{7,3},{8,12},{9,13},{10,... | collective-permute-start | bytes 258056 | tf_op jit(solution)/shard_map/ppermute | solution.py:341
  65.7 10.2 %collective-permute-start.3 = (f32[168,128]{1,0:T(8,128)S(1)}, f32[168,128]{1,0:T(8,128)S(1)}, u32[]{:S(2)}, u32[]{:S(2)}) collective-permute-start(f32[168,128]{1,0:T(8,128)S(1)} %add.36), channel_id=1, source_target_pairs={{0,3},{1,0},{2,1},{3,2},{4,7},{5,4},{6,5},{7,6},{8,11},{9,8},{10,9... | collective-permute-start | bytes 258056 | tf_op jit(solution)/shard_map/ppermute | solution.py:332
  67.2 8.7 %collective-permute-start.2 = (f32[168,128]{1,0:T(8,128)S(1)}, f32[168,128]{1,0:T(8,128)S(1)}, u32[]{:S(2)}, u32[]{:S(2)}) collective-permute-start(f32[168,128]{1,0:T(8,128)S(1)} %add.36), channel_id=1, source_target_pairs={{0,1},{1,2},{2,3},{3,0},{4,5},{5,6},{6,7},{7,4},{8,9},{9,10},{10,1... | collective-permute-start | bytes 258056 | tf_op jit(solution)/shard_map/ppermute | solution.py:332
  67.8 8.1 %collective-permute-start.1 = (f32[168,128]{1,0:T(8,128)S(1)}, f32[168,128]{1,0:T(8,128)S(1)}, u32[]{:S(2)}, u32[]{:S(2)}) collective-permute-start(f32[168,128]{1,0:T(8,128)S(1)} %add.36), channel_id=1, source_target_pairs={{0,2},{1,3},{2,0},{3,1},{4,6},{5,7},{6,4},{7,5},{8,10},{9,11},{10,... | collective-permute-start | bytes 258056 | tf_op jit(solution)/shard_map/ppermute | solution.py:332
  70.1 28.4 %all-to-all-start.2 = ((f32[64,16,128]{2,1,0:T(8,128)}), f32[64,16,128]{2,1,0:T(8,128)S(1)}, u32[]{:S(2)}, u32[]{:S(2)}) async-start(f32[64,16,128]{2,1,0:T(8,128)} %bitcast.6), calls=%async_computation.2 | async-start | bytes 1048576 | tf_op jit(solution)/shard_map/all_to_all | solution.py:345
  75.9 9.5 %collective-permute-start.6 = (f32[168,128]{1,0:T(8,128)S(1)}, f32[168,128]{1,0:T(8,128)S(1)}, u32[]{:S(2)}, u32[]{:S(2)}) collective-permute-start(f32[168,128]{1,0:T(8,128)S(1)} %add_add_fusion.1), channel_id=1, source_target_pairs={{0,24},{1,25},{2,26},{3,27},{4,28},{5,29},{6,30},{7,31},{8,0},{9,1... | collective-permute-start | bytes 258056 | tf_op jit(solution)/shard_map/ppermute | solution.py:332
  78.8 8.7 %collective-permute-start.5 = (f32[168,128]{1,0:T(8,128)S(1)}, f32[168,128]{1,0:T(8,128)S(1)}, u32[]{:S(2)}, u32[]{:S(2)}) collective-permute-start(f32[168,128]{1,0:T(8,128)S(1)} %add_add_fusion.1), channel_id=1, source_target_pairs={{0,8},{1,9},{2,10},{3,11},{4,12},{5,13},{6,14},{7,15},{8,16},{9,17... | collective-permute-start | bytes 258056 | tf_op jit(solution)/shard_map/ppermute | solution.py:332
  78.8 9.7 %collective-permute-start.4 = (f32[168,128]{1,0:T(8,128)S(1)}, f32[168,128]{1,0:T(8,128)S(1)}, u32[]{:S(2)}, u32[]{:S(2)}) collective-permute-start(f32[168,128]{1,0:T(8,128)S(1)} %add_add_fusion.1), channel_id=1, source_target_pairs={{0,16},{1,17},{2,18},{3,19},{4,20},{5,21},{6,22},{7,23},{8,24},{9,... | collective-permute-start | bytes 258056 | tf_op jit(solution)/shard_map/ppermute | solution.py:332
  88.5 6.3 %collective-permute-start.9 = (f32[168,128]{1,0:T(8,128)S(1)}, f32[168,128]{1,0:T(8,128)S(1)}, u32[]{:S(2)}, u32[]{:S(2)}) collective-permute-start(f32[168,128]{1,0:T(8,128)S(1)} %add_add_fusion.first), channel_id=1, source_target_pairs={{0,96},{1,97},{2,98},{3,99},{4,100},{5,101},{6,102},{7,103},{8,104... | collective-permute-start | bytes 258056 | tf_op jit(solution)/shard_map/ppermute | solution.py:332
  91.5 6.0 %collective-permute-start.8 = (f32[168,128]{1,0:T(8,128)S(1)}, f32[168,128]{1,0:T(8,128)S(1)}, u32[]{:S(2)}, u32[]{:S(2)}) collective-permute-start(f32[168,128]{1,0:T(8,128)S(1)} %add_add_fusion.first), channel_id=1, source_target_pairs={{0,64},{1,65},{2,66},{3,67},{4,68},{5,69},{6,70},{7,71},{8,72},{9,... | collective-permute-start | bytes 258056 | tf_op jit(solution)/shard_map/ppermute | solution.py:332
  92.2 6.3 %collective-permute-start.7 = (f32[168,128]{1,0:T(8,128)S(1)}, f32[168,128]{1,0:T(8,128)S(1)}, u32[]{:S(2)}, u32[]{:S(2)}) collective-permute-start(f32[168,128]{1,0:T(8,128)S(1)} %add_add_fusion.first), channel_id=1, source_target_pairs={{0,32},{1,33},{2,34},{3,35},{4,36},{5,37},{6,38},{7,39},{8,40},{9,... | collective-permute-start | bytes 258056 | tf_op jit(solution)/shard_map/ppermute | solution.py:332

commit v3 on v2

--- a/solution.py
+++ b/solution.py
@@ -15,6 +15,7 @@
 AXES = ("z", "y", "core", "x")
 CHIPS = ("z", "y", "x")
 BLOCK = 512
+WIDE = 1024
 LANES = 128
 F32 = jnp.float32
 BF16 = jnp.bfloat16
@@ -85,7 +86,7 @@
 
 
 def members(id_column):
-    labels = iota((BLOCK, STRATA), 1).astype(F32)
+    labels = iota(id_column.shape, 1).astype(F32)
     return jnp.where(id_column == labels, 1.0, 0.0).astype(BF16)
 
 
@@ -205,13 +206,13 @@
     pairs = jnp.zeros((4 * groups, LANES), F32)
     curvature = jnp.zeros((width, width), F32)
     gradient = jnp.zeros((1, width), F32)
-    for start in range(0, records, BLOCK):
-        span = pl.ds(start, BLOCK)
+    for start in range(0, records, WIDE):
+        span = pl.ds(start, WIDE)
         ids, owners, rows = strata[:, span], centers[:, span], covars[span, :]
         increment = q_in[:, span]
         hazard = hazard_in[:, span] + look_up(table, ids >> 7, one_hot(ids & 127, LANES), 8)
         exposure = w_in[:, span] * hazard
-        live = iota((1, BLOCK), 1) + start < counts[0]
+        live = iota((1, WIDE), 1) + start < counts[0]
         happened = jnp.where(live & (events[:, span] > 0), 1.0, 0.0)
         parts = split3(exposure)
         top = ids & ~255
@@ -224,7 +225,7 @@
         low_out[span, :] = mean_low
         flags = mxu(stack([happened], 8), rows)
         gradient = gradient + flags[:1] - jnp.sum(mean, axis=0, keepdims=True)
-        at = iota((groups, BLOCK), 0)
+        at = iota((groups, WIDE), 0)
         chosen = [jnp.where(at == owners >> 7, part, 0.0) for part in (*parts, happened)]
         pairs = pairs + mxu(
             jnp.concatenate(chosen, axis=0).astype(BF16), one_hot(owners & 127, LANES), NT
@@ -260,11 +261,11 @@
 
 
 def last_kernel(
-    load, devices, mine, first, second, third, fourth, shares, frailty,
+    load, devices, mine, first, second, shares, frailty,
     info, score, center_score, center_info, center_cross,
 ):
     width = info.shape[0]
-    pack = (first[...] + third[...]) + (second[...] + fourth[...])
+    pack = first[...] + second[...]
     total = load * CENTERS_DEV * devices
     root = math.sqrt(load)
     info[...] = pack[:width] / total
@@ -378,14 +379,16 @@
     swapped = other_core(pack)
     half = shaped(center_total // 2, width)
     core_zero, core_one = call(cross_kernel, (half, half), near=False)(centers, loaded)
-    pack = sum_ring(pack + swapped, "x")
+    pack = sum_ring(pack + swapped, "z")
     is_one = lax.axis_index("core") == 1
     keep = jnp.where(is_one, core_one, core_zero)
     give = jnp.where(is_one, core_zero, core_one)
     cross = keep + other_core(give)
     shares = exchange(cross.reshape(devices // 2, CENTERS_DEV, width), CHIPS)
     pack = sum_ring(pack, "y")
-    parts = gather_ring(pack, "z")
+    pack = pack + lax.ppermute(pack, AXES, moves(lambda z, y, c, x: (z, y, c, x ^ 1)))
+    other = lax.ppermute(pack, AXES, moves(lambda z, y, c, x: (z, y, c, x ^ 3)))
+    parts = [pack, other]
     last = call(
         functools.partial(last_kernel, records // CENTERS_DEV, devices),
         (

time: 99.7 us -> 99.6 us (level)
  waiting for transfers between devices: 31.3 us -> 33.4 us
  starting transfers between devices: 37.3 us -> 35.7 us
    ppermute x0 -> x2, waiting for transfers between devices: none -> 7.41 us  [the longest x1 3.83 us: body(): other = lax.ppermute(pack, AXES, moves(lambda z, y, c, x: (z, y, c, x ^ 3)))]
    ppermute x9 -> x6, waiting for transfers between devices: 12.7 us -> 7.39 us  [gather_ring(): lax.ppermute(value, AXES, moves(ahead(k)))]
    ppermute x9 -> x6, starting transfers between devices: 13.3 us -> 8.81 us  [gather_ring(): lax.ppermute(value, AXES, moves(ahead(k)))]
    ppermute x0 -> x2, starting transfers between devices: none -> 2.93 us  [the longest x1 1.94 us: body(): other = lax.ppermute(pack, AXES, moves(lambda z, y, c, x: (z, y, c, x ^ 3)))]
  transfers between devices with their start and end apart: 14 -> 13, of which waited for: 9 -> 8; matrix products, arithmetic and copies ran while one was open for 1% -> 1% of each run, Pallas kernels for 8% -> 8%
where the time goes in v3:
time: 99.6 us; the launch traced here: 99.1 us
  starting transfers between devices  35.7 us (36%)
  waiting for transfers between devices  33.4 us (34%)
  Pallas kernels  26.6 us (27%)
  between operations  1.56 us (2%)
  other arithmetic  1.01 us (1%)
    pallas_call x7, Pallas kernels, run(): pl.pallas_call(kernel, out_shape=out_shape, in_specs=[pl.BlockSpec(memory...  26.6 us
    all_to_all x3, starting transfers between devices, exchange(): return lax.all_to_all(value, axes, 0, 0, tiled=True)  23.4 us
    all_to_all x3, waiting for transfers between devices, exchange(): return lax.all_to_all(value, axes, 0, 0, tiled=True)  17.1 us
    ppermute x6, starting transfers between devices, gather_ring(): lax.ppermute(value, AXES, moves(ahead(k)))  8.81 us
    ppermute x6, waiting for transfers between devices, gather_ring(): lax.ppermute(value, AXES, moves(ahead(k)))  7.39 us
    ppermute x1, waiting for transfers between devices, body(): other = lax.ppermute(pack, AXES, moves(lambda z, y, c, x: (z, y, c, x ^ 3)))  3.83 us
    ppermute x1, waiting for transfers between devices, body(): lax.ppermute(pack, AXES, moves(lambda z, y, c, x: (z, y, c, x ^ 1)))  3.57 us
  transfers between devices with their start and end apart: 13, of which 8 were waited for; matrix products, arithmetic and copies ran while one was open for 1% of the time, Pallas kernels for 8%

profile of v3, /device:TPU:0, one launch (start us, length us, event | category | flops | bytes accessed | tf_op | source)
XLA Modules:
  0.0 99.1 jit_solution(5868593500897551201)
XLA Ops:
  1.4 6.0 %shard_map.110 = (f32[1,4096]{1,0:T(1,128)S(1)}, f32[128,8,128]{2,1,0:T(8,128)}) custom-call(s32[1]{0:T(128)S(6)} %copy.12.counts, s32[1,4096]{1,0:T(1,128)} %bitcast.10, s32[1,4096]{1,0:T(1,128)} %bitcast.15, f32[1,128]{1,0:T(1,128)} %bitcast.22, f32[16,128]{1,0:T(8,128)} %bitcast.20, bf16[4096,128]{1,0:T(8,128)(2,1)} %covars.5), custom_call_target="tpu_custom_call" | custom-call | tf_op jit(solution)/shard_map/pallas_call | solution.py:292
  7.4 11.7 %all-to-all-start = ((f32[128,8,128]{2,1,0:T(8,128)}), f32[128,8,128]{2,1,0:T(8,128)}, u32[]{:S(2)}, u32[]{:S(2)}) async-start(f32[128,8,128]{2,1,0:T(8,128)} %get-tuple-element.22), calls=%async_computation | async-start | bytes 1048576 | tf_op jit(solution)/shard_map/all_to_all | solution.py:346
  19.1 6.3 %shard_map.111 = (f32[1,4096]{1,0:T(1,128)S(1)}, f32[4096,128]{1,0:T(8,128)S(1)}) custom-call(s32[1,4096]{1,0:T(1,128)S(1)} %bitcast.11, f32[1,4096]{1,0:T(1,128)S(1)} %get-tuple-element.20.w_in, bf16[4096,128]{1,0:T(8,128)(2,1)S(1)} %copy-done), custom_call_target="tpu_custom_call" | custom-call | tf_op jit(solution)/shard_map/pallas_call | solution.py:292
  25.4 6.4 %all-to-all-done.received = f32[128,8,128]{2,1,0:T(8,128)} async-done(((f32[128,8,128]{2,1,0:T(8,128)}), f32[128,8,128]{2,1,0:T(8,128)}, u32[]{:S(2)}, u32[]{:S(2)}) %all-to-all-start) | async-done | bytes 524320 | tf_op jit(solution)/shard_map/all_to_all | solution.py:346
  31.9 2.3 %shard_map.112 = (f32[1,4096]{1,0:T(1,128)S(1)}, f32[128,8,128]{2,1,0:T(8,128)S(1)}) custom-call(s32[1]{0:T(128)S(6)} %copy.12.counts, s32[1]{0:T(128)} %bitcast.mine, s32[1,4096]{1,0:T(1,128)S(1)} %bitcast.12, s32[1,4096]{1,0:T(1,128)S(1)} %bitcast.18, f32[1,4096]{1,0:T(1,128)S(1)} %get-tuple-element.21.zero_in, f32[128,8,128]{2,1,0:T(8,128)} %all-to-all-done.received), custom_call_target="tpu_custom_call" | custom-call | tf_op jit(solution)/shard_map/pallas_call | solution.py:292
  35.0 5.9 %all-to-all-start.1 = ((f32[128,8,128]{2,1,0:T(8,128)}), f32[128,8,128]{2,1,0:T(8,128)}, u32[]{:S(2)}, u32[]{:S(2)}) async-start(f32[128,8,128]{2,1,0:T(8,128)} %copy-done.1), calls=%async_computation.1 | async-start | bytes 1048576 | tf_op jit(solution)/shard_map/all_to_all | solution.py:346
  40.9 1.9 %shard_map.113.hazard_in = f32[1,4096]{1,0:T(1,128)S(1)} custom-call(s32[1,4096]{1,0:T(1,128)S(1)} %bitcast.13, f32[1,4096]{1,0:T(1,128)S(1)} %get-tuple-element.23.q_in), custom_call_target="tpu_custom_call" | custom-call | tf_op jit(solution)/shard_map/pallas_call | solution.py:292
  42.9 10.7 %all-to-all-done.1.received = f32[128,8,128]{2,1,0:T(8,128)} async-done(((f32[128,8,128]{2,1,0:T(8,128)}), f32[128,8,128]{2,1,0:T(8,128)}, u32[]{:S(2)}, u32[]{:S(2)}) %all-to-all-start.1) | async-done | bytes 524320 | tf_op jit(solution)/shard_map/all_to_all | solution.py:346
  53.6 5.5 %shard_map.114 = (bf16[4096,128]{1,0:T(8,128)(2,1)}, f32[168,128]{1,0:T(8,128)S(1)}) custom-call(s32[1]{0:T(128)S(6)} %copy.12.counts, s32[1]{0:T(128)} %bitcast.mine, s32[1,4096]{1,0:T(1,128)S(1)} %bitcast.14, s32[1,4096]{1,0:T(1,128)S(1)} %bitcast.17, s32[1,4096]{1,0:T(1,128)S(1)} %bitcast.19, f32[1,4096]{1,0:T(1,128)S(1)} %get-tuple-element.20.w_in, ...), custom_call_target="tpu_custom_call" | custom-call | tf_op jit(solution)/shard_map/pallas_call | solution.py:292
  59.0 3.9 %shard_map.115 = (f32[1024,128]{1,0:T(8,128)S(1)}, f32[1024,128]{1,0:T(8,128)S(1)}) custom-call(s32[1,4096]{1,0:T(1,128)} %bitcast.16, bf16[4096,128]{1,0:T(8,128)(2,1)} %get-tuple-element.27.loaded), custom_call_target="tpu_custom_call" | custom-call | tf_op jit(solution)/shard_map/pallas_call | solution.py:292
  63.6 1.5 %collective-permute-done = f32[168,128]{1,0:T(8,128)S(1)} collective-permute-done((f32[168,128]{1,0:T(8,128)S(1)}, f32[168,128]{1,0:T(8,128)S(1)}, u32[]{:S(2)}, u32[]{:S(2)}) %collective-permute-start) | collective-permute-done | bytes 86048 | tf_op jit(solution)/shard_map/ppermute | solution.py:342
  65.1 0.9 collective-permute-start.3
  66.1 1.2 %collective-permute-start.2 = (f32[168,128]{1,0:T(8,128)S(1)}, f32[168,128]{1,0:T(8,128)S(1)}, u32[]{:S(2)}, u32[]{:S(2)}) collective-permute-start(f32[168,128]{1,0:T(8,128)S(1)} %add.39), channel_id=1, source_target_pairs={{0,32},{1,33},{2,34},{3,35},{4,36},{5,37},{6,38},{7,39},{8,40},{9,... | collective-permute-start | bytes 258056 | tf_op jit(solution)/shard_map/ppermute | solution.py:333
  67.2 1.5 %collective-permute-start.1 = (f32[168,128]{1,0:T(8,128)S(1)}, f32[168,128]{1,0:T(8,128)S(1)}, u32[]{:S(2)}, u32[]{:S(2)}) collective-permute-start(f32[168,128]{1,0:T(8,128)S(1)} %add.39), channel_id=1, source_target_pairs={{0,64},{1,65},{2,66},{3,67},{4,68},{5,69},{6,70},{7,71},{8,72},{9,... | collective-permute-start | bytes 258056 | tf_op jit(solution)/shard_map/ppermute | solution.py:333
  69.7 5.8 %all-to-all-start.2 = ((f32[64,16,128]{2,1,0:T(8,128)}), f32[64,16,128]{2,1,0:T(8,128)S(1)}, u32[]{:S(2)}, u32[]{:S(2)}) async-start(f32[64,16,128]{2,1,0:T(8,128)} %bitcast.6), calls=%async_computation.2 | async-start | bytes 1048576 | tf_op jit(solution)/shard_map/all_to_all | solution.py:346
  75.5 2.9 %collective-permute-start.6 = (f32[168,128]{1,0:T(8,128)S(1)}, f32[168,128]{1,0:T(8,128)S(1)}, u32[]{:S(2)}, u32[]{:S(2)}) collective-permute-start(f32[168,128]{1,0:T(8,128)S(1)} %add_add_fusion.1), channel_id=1, source_target_pairs={{0,24},{1,25},{2,26},{3,27},{4,28},{5,29},{6,30},{7,31},{8,0},{9,1... | collective-permute-start | bytes 258056 | tf_op jit(solution)/shard_map/ppermute | solution.py:333
  78.4 2.3 %collective-permute-start.4 = (f32[168,128]{1,0:T(8,128)S(1)}, f32[168,128]{1,0:T(8,128)S(1)}, u32[]{:S(2)}, u32[]{:S(2)}) collective-permute-start(f32[168,128]{1,0:T(8,128)S(1)} %add_add_fusion.1), channel_id=1, source_target_pairs={{0,16},{1,17},{2,18},{3,19},{4,20},{5,21},{6,22},{7,23},{8,24},{9,... | collective-permute-start | bytes 258056 | tf_op jit(solution)/shard_map/ppermute | solution.py:333
  80.7 4.3 %collective-permute-done.6 = f32[168,128]{1,0:T(8,128)S(1)} collective-permute-done((f32[168,128]{1,0:T(8,128)S(1)}, f32[168,128]{1,0:T(8,128)S(1)}, u32[]{:S(2)}, u32[]{:S(2)}) %collective-permute-start.6) | collective-permute-done | bytes 86048 | tf_op jit(solution)/shard_map/ppermute | solution.py:333
  85.0 2.1 %collective-permute-done.5 = f32[168,128]{1,0:T(8,128)S(1)} collective-permute-done((f32[168,128]{1,0:T(8,128)S(1)}, f32[168,128]{1,0:T(8,128)S(1)}, u32[]{:S(2)}, u32[]{:S(2)}) %collective-permute-start.5) | collective-permute-done | bytes 86048 | tf_op jit(solution)/shard_map/ppermute | solution.py:333
  87.1 1.0 collective-permute-done.4
  88.1 1.0 collective-permute-start.7
  89.1 3.6 %collective-permute-done.7 = f32[168,128]{1,0:T(8,128)S(1)} collective-permute-done((f32[168,128]{1,0:T(8,128)S(1)}, f32[168,128]{1,0:T(8,128)S(1)}, u32[]{:S(2)}, u32[]{:S(2)}) %collective-permute-start.7) | collective-permute-done | bytes 86048 | tf_op jit(solution)/shard_map/ppermute | solution.py:389
  92.7 1.9 %collective-permute-start.8 = (f32[168,128]{1,0:T(8,128)S(1)}, f32[168,128]{1,0:T(8,128)S(1)}, u32[]{:S(2)}, u32[]{:S(2)}) collective-permute-start(f32[168,128]{1,0:T(8,128)S(1)} %add.46.first), channel_id=1, source_target_pairs={{0,3},{1,2},{2,1},{3,0},{4,7},{5,6},{6,5},{7,4},{8,11},{9,10},{10,... | collective-permute-start | bytes 258056 | tf_op jit(solution)/shard_map/ppermute | solution.py:390
  94.6 3.8 %collective-permute-done.8.second = f32[168,128]{1,0:T(8,128)S(1)} collective-permute-done((f32[168,128]{1,0:T(8,128)S(1)}, f32[168,128]{1,0:T(8,128)S(1)}, u32[]{:S(2)}, u32[]{:S(2)}) %collective-permute-start.8) | collective-permute-done | bytes 86048 | tf_op jit(solution)/shard_map/ppermute | solution.py:390
  (27 shorter events, 3.1 us)
Async XLA Ops:
  0.6 18.4 %copy-start = (bf16[4096,128]{1,0:T(8,128)(2,1)S(1)}, bf16[4096,128]{1,0:T(8,128)(2,1)}, u32[]{:S(2)}) copy-start(bf16[4096,128]{1,0:T(8,128)(2,1)} %covars.5) | copy-start | bytes 3145732
  0.6 18.4 %copy-start.2 = (s32[4096]{0:T(1024)S(1)}, s32[4096]{0:T(1024)}, u32[]{:S(2)}) copy-start(s32[4096]{0:T(1024)} %param.8) | copy-start | bytes 49156
  0.7 31.2 %copy-start.4 = (s32[4096]{0:T(1024)S(1)}, s32[4096]{0:T(1024)}, u32[]{:S(2)}) copy-start(s32[4096]{0:T(1024)} %param.10) | copy-start | bytes 49156
  7.3 46.2 %copy-start.3 = (s32[4096]{0:T(1024)S(1)}, s32[4096]{0:T(1024)}, u32[]{:S(2)}) copy-start(s32[4096]{0:T(1024)} %param.9) | copy-start | bytes 49156
  7.4 24.5 %all-to-all-start = ((f32[128,8,128]{2,1,0:T(8,128)}), f32[128,8,128]{2,1,0:T(8,128)}, u32[]{:S(2)}, u32[]{:S(2)}) async-start(f32[128,8,128]{2,1,0:T(8,128)} %get-tuple-element.22), calls=%async_computation | async-start | bytes 1048576 | tf_op jit(solution)/shard_map/all_to_all | solution.py:346
  34.2 0.8 copy-start.1
  35.0 18.5 %all-to-all-start.1 = ((f32[128,8,128]{2,1,0:T(8,128)}), f32[128,8,128]{2,1,0:T(8,128)}, u32[]{:S(2)}, u32[]{:S(2)}) async-start(f32[128,8,128]{2,1,0:T(8,128)} %copy-done.1), calls=%async_computation.1 | async-start | bytes 1048576 | tf_op jit(solution)/shard_map/all_to_all | solution.py:346
  63.0 5.8 %collective-permute-start.9 = (f32[1024,128]{1,0:T(8,128)S(1)}, f32[1024,128]{1,0:T(8,128)S(1)}, u32[]{:S(2)}, u32[]{:S(2)}) collective-permute-start(f32[1024,128]{1,0:T(8,128)S(1)} %broadcast_select_fusion), channel_id=1, source_target_pairs={{0,4},{1,5},{2,6},{3,7},{4,0},{5,1},{6,2},{7,3},{8,12},{9,13},{10,... | collective-permute-start | bytes 1572872 | tf_op jit(solution)/shard_map/ppermute | solution.py:342
  63.2 1.9 %collective-permute-start = (f32[168,128]{1,0:T(8,128)S(1)}, f32[168,128]{1,0:T(8,128)S(1)}, u32[]{:S(2)}, u32[]{:S(2)}) collective-permute-start(f32[168,128]{1,0:T(8,128)S(1)} %get-tuple-element.26), channel_id=1, source_target_pairs={{0,4},{1,5},{2,6},{3,7},{4,0},{5,1},{6,2},{7,3},{8,12},{9,13},{10,... | collective-permute-start | bytes 258056 | tf_op jit(solution)/shard_map/ppermute | solution.py:342
  65.1 33.3 %copy-start.5 = (f32[2048]{0:T(1024)S(1)}, f32[2048]{0:T(1024)}, u32[]{:S(2)}) copy-start(f32[2048]{0:T(1024)} %param.13) | copy-start | bytes 24580
  65.1 10.3 %collective-permute-start.3 = (f32[168,128]{1,0:T(8,128)S(1)}, f32[168,128]{1,0:T(8,128)S(1)}, u32[]{:S(2)}, u32[]{:S(2)}) collective-permute-start(f32[168,128]{1,0:T(8,128)S(1)} %add.39), channel_id=1, source_target_pairs={{0,96},{1,97},{2,98},{3,99},{4,100},{5,101},{6,102},{7,103},{8,104... | collective-permute-start | bytes 258056 | tf_op jit(solution)/shard_map/ppermute | solution.py:333
  66.1 9.4 %collective-permute-start.2 = (f32[168,128]{1,0:T(8,128)S(1)}, f32[168,128]{1,0:T(8,128)S(1)}, u32[]{:S(2)}, u32[]{:S(2)}) collective-permute-start(f32[168,128]{1,0:T(8,128)S(1)} %add.39), channel_id=1, source_target_pairs={{0,32},{1,33},{2,34},{3,35},{4,36},{5,37},{6,38},{7,39},{8,40},{9,... | collective-permute-start | bytes 258056 | tf_op jit(solution)/shard_map/ppermute | solution.py:333
  67.2 8.2 %collective-permute-start.1 = (f32[168,128]{1,0:T(8,128)S(1)}, f32[168,128]{1,0:T(8,128)S(1)}, u32[]{:S(2)}, u32[]{:S(2)}) collective-permute-start(f32[168,128]{1,0:T(8,128)S(1)} %add.39), channel_id=1, source_target_pairs={{0,64},{1,65},{2,66},{3,67},{4,68},{5,69},{6,70},{7,71},{8,72},{9,... | collective-permute-start | bytes 258056 | tf_op jit(solution)/shard_map/ppermute | solution.py:333
  69.7 28.8 %all-to-all-start.2 = ((f32[64,16,128]{2,1,0:T(8,128)}), f32[64,16,128]{2,1,0:T(8,128)S(1)}, u32[]{:S(2)}, u32[]{:S(2)}) async-start(f32[64,16,128]{2,1,0:T(8,128)} %bitcast.6), calls=%async_computation.2 | async-start | bytes 1048576 | tf_op jit(solution)/shard_map/all_to_all | solution.py:346
  75.5 9.5 %collective-permute-start.6 = (f32[168,128]{1,0:T(8,128)S(1)}, f32[168,128]{1,0:T(8,128)S(1)}, u32[]{:S(2)}, u32[]{:S(2)}) collective-permute-start(f32[168,128]{1,0:T(8,128)S(1)} %add_add_fusion.1), channel_id=1, source_target_pairs={{0,24},{1,25},{2,26},{3,27},{4,28},{5,29},{6,30},{7,31},{8,0},{9,1... | collective-permute-start | bytes 258056 | tf_op jit(solution)/shard_map/ppermute | solution.py:333
  78.3 8.7 %collective-permute-start.5 = (f32[168,128]{1,0:T(8,128)S(1)}, f32[168,128]{1,0:T(8,128)S(1)}, u32[]{:S(2)}, u32[]{:S(2)}) collective-permute-start(f32[168,128]{1,0:T(8,128)S(1)} %add_add_fusion.1), channel_id=1, source_target_pairs={{0,8},{1,9},{2,10},{3,11},{4,12},{5,13},{6,14},{7,15},{8,16},{9,17... | collective-permute-start | bytes 258056 | tf_op jit(solution)/shard_map/ppermute | solution.py:333
  78.4 9.7 %collective-permute-start.4 = (f32[168,128]{1,0:T(8,128)S(1)}, f32[168,128]{1,0:T(8,128)S(1)}, u32[]{:S(2)}, u32[]{:S(2)}) collective-permute-start(f32[168,128]{1,0:T(8,128)S(1)} %add_add_fusion.1), channel_id=1, source_target_pairs={{0,16},{1,17},{2,18},{3,19},{4,20},{5,21},{6,22},{7,23},{8,24},{9,... | collective-permute-start | bytes 258056 | tf_op jit(solution)/shard_map/ppermute | solution.py:333
  88.1 4.6 %collective-permute-start.7 = (f32[168,128]{1,0:T(8,128)S(1)}, f32[168,128]{1,0:T(8,128)S(1)}, u32[]{:S(2)}, u32[]{:S(2)}) collective-permute-start(f32[168,128]{1,0:T(8,128)S(1)} %add_add_fusion), channel_id=1, source_target_pairs={{0,1},{1,0},{2,3},{3,2},{4,5},{5,4},{6,7},{7,6},{8,9},{9,8},{10,11... | collective-permute-start | bytes 258056 | tf_op jit(solution)/shard_map/ppermute | solution.py:389
  92.7 5.8 %collective-permute-start.8 = (f32[168,128]{1,0:T(8,128)S(1)}, f32[168,128]{1,0:T(8,128)S(1)}, u32[]{:S(2)}, u32[]{:S(2)}) collective-permute-start(f32[168,128]{1,0:T(8,128)S(1)} %add.46.first), channel_id=1, source_target_pairs={{0,3},{1,2},{2,1},{3,0},{4,7},{5,6},{6,5},{7,4},{8,11},{9,10},{10,... | collective-permute-start | bytes 258056 | tf_op jit(solution)/shard_map/ppermute | solution.py:390

commit v4 on v3

--- a/solution.py
+++ b/solution.py
@@ -16,6 +16,7 @@
 CHIPS = ("z", "y", "x")
 BLOCK = 512
 WIDE = 1024
+ALL = 4096
 LANES = 128
 F32 = jnp.float32
 BF16 = jnp.bfloat16
@@ -100,13 +101,13 @@
     table = table_rows(frailty[...])
     total_zero = jnp.zeros((8, LANES), F32)
     total_one = jnp.zeros((STRATA, LANES), F32)
-    for start in range(0, records, BLOCK):
-        span = pl.ds(start, BLOCK)
+    for start in range(0, records, WIDE):
+        span = pl.ds(start, WIDE)
         ids, owners, rows = strata[:, span], centers[:, span], covars[span, :]
         eta = jnp.sum(mxu(betas, rows, NT), axis=0, keepdims=True) + look_up(
             table, owners >> 7, one_hot(owners & 127, LANES), frailty.shape[0]
         )
-        live = iota((1, BLOCK), 1) + start < counts[0]
+        live = iota((1, WIDE), 1) + start < counts[0]
         weight = jnp.where(live, jnp.exp(eta), 0.0)
         w_out[:, span] = weight
         weighted = (columns(split3(weight)) * rows.astype(F32)).astype(BF16)
@@ -154,12 +155,12 @@
         running = running + received[slab, :]
     table = table_rows(later[pl.ds(pl.multiple_of(mine[0] * 8, 8), 8), :])
     total = jnp.zeros((8, LANES), F32)
-    for start in range(0, records, BLOCK):
-        span = pl.ds(start, BLOCK)
+    for start in range(0, records, ALL):
+        span = pl.ds(start, ALL)
         ids = strata[:, span]
         lower_hot = one_hot(ids & 127, LANES)
         zero = zero_in[:, span] + look_up(table, ids >> 7, lower_hot, 8)
-        live = iota((1, BLOCK), 1) + start < counts[0]
+        live = iota((1, ALL), 1) + start < counts[0]
         happened = live & (events[:, span] > 0)
         increment = jnp.where(happened, 1.0 / jnp.where(happened, zero, 1.0), 0.0)
         q_out[:, span] = increment

time: 99.6 us -> 98.6 us (0.990)
  Pallas kernels: 26.6 us -> 25.6 us
    pallas_call x7, Pallas kernels: 26.6 us -> 25.6 us  [run(): pl.pallas_call(kernel, out_shape=out_shape, in_specs=[pl.BlockSpec(memory...]
where the time goes in v4:
time: 98.6 us; the launch traced here: 98.1 us
  starting transfers between devices  35.7 us (36%)
  waiting for transfers between devices  33.4 us (34%)
  Pallas kernels  25.6 us (26%)
  between operations  1.56 us (2%)
  other arithmetic  1.01 us (1%)
    pallas_call x7, Pallas kernels, run(): pl.pallas_call(kernel, out_shape=out_shape, in_specs=[pl.BlockSpec(memory...  25.6 us
    all_to_all x3, starting transfers between devices, exchange(): return lax.all_to_all(value, axes, 0, 0, tiled=True)  23.4 us
    all_to_all x3, waiting for transfers between devices, exchange(): return lax.all_to_all(value, axes, 0, 0, tiled=True)  17.1 us
    ppermute x6, starting transfers between devices, gather_ring(): lax.ppermute(value, AXES, moves(ahead(k)))  8.81 us
    ppermute x6, waiting for transfers between devices, gather_ring(): lax.ppermute(value, AXES, moves(ahead(k)))  7.39 us
    ppermute x1, waiting for transfers between devices, body(): other = lax.ppermute(pack, AXES, moves(lambda z, y, c, x: (z, y, c, x ^ 3)))  3.83 us
    ppermute x1, waiting for transfers between devices, body(): lax.ppermute(pack, AXES, moves(lambda z, y, c, x: (z, y, c, x ^ 1)))  3.57 us
  transfers between devices with their start and end apart: 13, of which 8 were waited for; matrix products, arithmetic and copies ran while one was open for 1% of the time, Pallas kernels for 8%

profile of v4, /device:TPU:0, one launch (start us, length us, event | category | flops | bytes accessed | tf_op | source)
XLA Modules:
  0.0 98.1 jit_solution(13195156959114256309)
XLA Ops:
  1.4 5.2 %shard_map.110 = (f32[1,4096]{1,0:T(1,128)S(1)}, f32[128,8,128]{2,1,0:T(8,128)}) custom-call(s32[1]{0:T(128)S(6)} %copy.12.counts, s32[1,4096]{1,0:T(1,128)} %bitcast.10, s32[1,4096]{1,0:T(1,128)} %bitcast.15, f32[1,128]{1,0:T(1,128)} %bitcast.22, f32[16,128]{1,0:T(8,128)} %bitcast.20, bf16[4096,128]{1,0:T(8,128)(2,1)} %covars.5), custom_call_target="tpu_custom_call" | custom-call | tf_op jit(solution)/shard_map/pallas_call | solution.py:293
  6.6 11.7 %all-to-all-start = ((f32[128,8,128]{2,1,0:T(8,128)}), f32[128,8,128]{2,1,0:T(8,128)}, u32[]{:S(2)}, u32[]{:S(2)}) async-start(f32[128,8,128]{2,1,0:T(8,128)} %get-tuple-element.22), calls=%async_computation | async-start | bytes 1048576 | tf_op jit(solution)/shard_map/all_to_all | solution.py:347
  18.3 6.3 %shard_map.111 = (f32[1,4096]{1,0:T(1,128)S(1)}, f32[4096,128]{1,0:T(8,128)S(1)}) custom-call(s32[1,4096]{1,0:T(1,128)S(1)} %bitcast.11, f32[1,4096]{1,0:T(1,128)S(1)} %get-tuple-element.20.w_in, bf16[4096,128]{1,0:T(8,128)(2,1)S(1)} %copy-done), custom_call_target="tpu_custom_call" | custom-call | tf_op jit(solution)/shard_map/pallas_call | solution.py:293
  24.6 6.4 %all-to-all-done.received = f32[128,8,128]{2,1,0:T(8,128)} async-done(((f32[128,8,128]{2,1,0:T(8,128)}), f32[128,8,128]{2,1,0:T(8,128)}, u32[]{:S(2)}, u32[]{:S(2)}) %all-to-all-start) | async-done | bytes 524320 | tf_op jit(solution)/shard_map/all_to_all | solution.py:347
  31.1 2.1 %shard_map.112 = (f32[1,4096]{1,0:T(1,128)S(1)}, f32[128,8,128]{2,1,0:T(8,128)S(1)}) custom-call(s32[1]{0:T(128)S(6)} %copy.12.counts, s32[1]{0:T(128)} %bitcast.mine, s32[1,4096]{1,0:T(1,128)S(1)} %bitcast.12, s32[1,4096]{1,0:T(1,128)S(1)} %bitcast.18, f32[1,4096]{1,0:T(1,128)S(1)} %get-tuple-element.21.zero_in, f32[128,8,128]{2,1,0:T(8,128)} %all-to-all-done.received), custom_call_target="tpu_custom_call" | custom-call | tf_op jit(solution)/shard_map/pallas_call | solution.py:293
  34.0 5.9 %all-to-all-start.1 = ((f32[128,8,128]{2,1,0:T(8,128)}), f32[128,8,128]{2,1,0:T(8,128)}, u32[]{:S(2)}, u32[]{:S(2)}) async-start(f32[128,8,128]{2,1,0:T(8,128)} %copy-done.1), calls=%async_computation.1 | async-start | bytes 1048576 | tf_op jit(solution)/shard_map/all_to_all | solution.py:347
  39.9 1.9 %shard_map.113.hazard_in = f32[1,4096]{1,0:T(1,128)S(1)} custom-call(s32[1,4096]{1,0:T(1,128)S(1)} %bitcast.13, f32[1,4096]{1,0:T(1,128)S(1)} %get-tuple-element.23.q_in), custom_call_target="tpu_custom_call" | custom-call | tf_op jit(solution)/shard_map/pallas_call | solution.py:293
  41.8 10.7 %all-to-all-done.1.received = f32[128,8,128]{2,1,0:T(8,128)} async-done(((f32[128,8,128]{2,1,0:T(8,128)}), f32[128,8,128]{2,1,0:T(8,128)}, u32[]{:S(2)}, u32[]{:S(2)}) %all-to-all-start.1) | async-done | bytes 524320 | tf_op jit(solution)/shard_map/all_to_all | solution.py:347
  52.5 5.5 %shard_map.114 = (bf16[4096,128]{1,0:T(8,128)(2,1)}, f32[168,128]{1,0:T(8,128)S(1)}) custom-call(s32[1]{0:T(128)S(6)} %copy.12.counts, s32[1]{0:T(128)} %bitcast.mine, s32[1,4096]{1,0:T(1,128)S(1)} %bitcast.14, s32[1,4096]{1,0:T(1,128)S(1)} %bitcast.17, s32[1,4096]{1,0:T(1,128)S(1)} %bitcast.19, f32[1,4096]{1,0:T(1,128)S(1)} %get-tuple-element.20.w_in, ...), custom_call_target="tpu_custom_call" | custom-call | tf_op jit(solution)/shard_map/pallas_call | solution.py:293
  58.0 3.9 %shard_map.115 = (f32[1024,128]{1,0:T(8,128)S(1)}, f32[1024,128]{1,0:T(8,128)S(1)}) custom-call(s32[1,4096]{1,0:T(1,128)} %bitcast.16, bf16[4096,128]{1,0:T(8,128)(2,1)} %get-tuple-element.27.loaded), custom_call_target="tpu_custom_call" | custom-call | tf_op jit(solution)/shard_map/pallas_call | solution.py:293
  62.6 1.5 %collective-permute-done = f32[168,128]{1,0:T(8,128)S(1)} collective-permute-done((f32[168,128]{1,0:T(8,128)S(1)}, f32[168,128]{1,0:T(8,128)S(1)}, u32[]{:S(2)}, u32[]{:S(2)}) %collective-permute-start) | collective-permute-done | bytes 86048 | tf_op jit(solution)/shard_map/ppermute | solution.py:343
  64.1 0.9 collective-permute-start.3
  65.0 1.2 %collective-permute-start.2 = (f32[168,128]{1,0:T(8,128)S(1)}, f32[168,128]{1,0:T(8,128)S(1)}, u32[]{:S(2)}, u32[]{:S(2)}) collective-permute-start(f32[168,128]{1,0:T(8,128)S(1)} %add.39), channel_id=1, source_target_pairs={{0,32},{1,33},{2,34},{3,35},{4,36},{5,37},{6,38},{7,39},{8,40},{9,... | collective-permute-start | bytes 258056 | tf_op jit(solution)/shard_map/ppermute | solution.py:334
  66.2 1.5 %collective-permute-start.1 = (f32[168,128]{1,0:T(8,128)S(1)}, f32[168,128]{1,0:T(8,128)S(1)}, u32[]{:S(2)}, u32[]{:S(2)}) collective-permute-start(f32[168,128]{1,0:T(8,128)S(1)} %add.39), channel_id=1, source_target_pairs={{0,64},{1,65},{2,66},{3,67},{4,68},{5,69},{6,70},{7,71},{8,72},{9,... | collective-permute-start | bytes 258056 | tf_op jit(solution)/shard_map/ppermute | solution.py:334
  68.6 5.7 %all-to-all-start.2 = ((f32[64,16,128]{2,1,0:T(8,128)}), f32[64,16,128]{2,1,0:T(8,128)S(1)}, u32[]{:S(2)}, u32[]{:S(2)}) async-start(f32[64,16,128]{2,1,0:T(8,128)} %bitcast.6), calls=%async_computation.2 | async-start | bytes 1048576 | tf_op jit(solution)/shard_map/all_to_all | solution.py:347
  74.5 2.9 %collective-permute-start.6 = (f32[168,128]{1,0:T(8,128)S(1)}, f32[168,128]{1,0:T(8,128)S(1)}, u32[]{:S(2)}, u32[]{:S(2)}) collective-permute-start(f32[168,128]{1,0:T(8,128)S(1)} %add_add_fusion.1), channel_id=1, source_target_pairs={{0,24},{1,25},{2,26},{3,27},{4,28},{5,29},{6,30},{7,31},{8,0},{9,1... | collective-permute-start | bytes 258056 | tf_op jit(solution)/shard_map/ppermute | solution.py:334
  77.3 2.3 %collective-permute-start.4 = (f32[168,128]{1,0:T(8,128)S(1)}, f32[168,128]{1,0:T(8,128)S(1)}, u32[]{:S(2)}, u32[]{:S(2)}) collective-permute-start(f32[168,128]{1,0:T(8,128)S(1)} %add_add_fusion.1), channel_id=1, source_target_pairs={{0,16},{1,17},{2,18},{3,19},{4,20},{5,21},{6,22},{7,23},{8,24},{9,... | collective-permute-start | bytes 258056 | tf_op jit(solution)/shard_map/ppermute | solution.py:334
  79.6 4.3 %collective-permute-done.6 = f32[168,128]{1,0:T(8,128)S(1)} collective-permute-done((f32[168,128]{1,0:T(8,128)S(1)}, f32[168,128]{1,0:T(8,128)S(1)}, u32[]{:S(2)}, u32[]{:S(2)}) %collective-permute-start.6) | collective-permute-done | bytes 86048 | tf_op jit(solution)/shard_map/ppermute | solution.py:334
  84.0 2.1 %collective-permute-done.5 = f32[168,128]{1,0:T(8,128)S(1)} collective-permute-done((f32[168,128]{1,0:T(8,128)S(1)}, f32[168,128]{1,0:T(8,128)S(1)}, u32[]{:S(2)}, u32[]{:S(2)}) %collective-permute-start.5) | collective-permute-done | bytes 86048 | tf_op jit(solution)/shard_map/ppermute | solution.py:334
  86.0 1.0 collective-permute-done.4
  87.0 1.0 %collective-permute-start.7 = (f32[168,128]{1,0:T(8,128)S(1)}, f32[168,128]{1,0:T(8,128)S(1)}, u32[]{:S(2)}, u32[]{:S(2)}) collective-permute-start(f32[168,128]{1,0:T(8,128)S(1)} %add_add_fusion), channel_id=1, source_target_pairs={{0,1},{1,0},{2,3},{3,2},{4,5},{5,4},{6,7},{7,6},{8,9},{9,8},{10,11... | collective-permute-start | bytes 258056 | tf_op jit(solution)/shard_map/ppermute | solution.py:390
  88.0 3.6 %collective-permute-done.7 = f32[168,128]{1,0:T(8,128)S(1)} collective-permute-done((f32[168,128]{1,0:T(8,128)S(1)}, f32[168,128]{1,0:T(8,128)S(1)}, u32[]{:S(2)}, u32[]{:S(2)}) %collective-permute-start.7) | collective-permute-done | bytes 86048 | tf_op jit(solution)/shard_map/ppermute | solution.py:390
  91.6 1.9 %collective-permute-start.8 = (f32[168,128]{1,0:T(8,128)S(1)}, f32[168,128]{1,0:T(8,128)S(1)}, u32[]{:S(2)}, u32[]{:S(2)}) collective-permute-start(f32[168,128]{1,0:T(8,128)S(1)} %add.46.first), channel_id=1, source_target_pairs={{0,3},{1,2},{2,1},{3,0},{4,7},{5,6},{6,5},{7,4},{8,11},{9,10},{10,... | collective-permute-start | bytes 258056 | tf_op jit(solution)/shard_map/ppermute | solution.py:391
  93.6 3.8 %collective-permute-done.8.second = f32[168,128]{1,0:T(8,128)S(1)} collective-permute-done((f32[168,128]{1,0:T(8,128)S(1)}, f32[168,128]{1,0:T(8,128)S(1)}, u32[]{:S(2)}, u32[]{:S(2)}) %collective-permute-start.8) | collective-permute-done | bytes 86048 | tf_op jit(solution)/shard_map/ppermute | solution.py:391
  (27 shorter events, 3.1 us)
Async XLA Ops:
  0.6 17.7 %copy-start = (bf16[4096,128]{1,0:T(8,128)(2,1)S(1)}, bf16[4096,128]{1,0:T(8,128)(2,1)}, u32[]{:S(2)}) copy-start(bf16[4096,128]{1,0:T(8,128)(2,1)} %covars.5) | copy-start | bytes 3145732
  0.6 17.7 %copy-start.2 = (s32[4096]{0:T(1024)S(1)}, s32[4096]{0:T(1024)}, u32[]{:S(2)}) copy-start(s32[4096]{0:T(1024)} %param.8) | copy-start | bytes 49156
  0.7 30.4 %copy-start.4 = (s32[4096]{0:T(1024)S(1)}, s32[4096]{0:T(1024)}, u32[]{:S(2)}) copy-start(s32[4096]{0:T(1024)} %param.10) | copy-start | bytes 49156
  6.6 46.0 %copy-start.3 = (s32[4096]{0:T(1024)S(1)}, s32[4096]{0:T(1024)}, u32[]{:S(2)}) copy-start(s32[4096]{0:T(1024)} %param.9) | copy-start | bytes 49156
  6.6 24.5 %all-to-all-start = ((f32[128,8,128]{2,1,0:T(8,128)}), f32[128,8,128]{2,1,0:T(8,128)}, u32[]{:S(2)}, u32[]{:S(2)}) async-start(f32[128,8,128]{2,1,0:T(8,128)} %get-tuple-element.22), calls=%async_computation | async-start | bytes 1048576 | tf_op jit(solution)/shard_map/all_to_all | solution.py:347
  33.2 0.8 copy-start.1
  34.0 18.5 %all-to-all-start.1 = ((f32[128,8,128]{2,1,0:T(8,128)}), f32[128,8,128]{2,1,0:T(8,128)}, u32[]{:S(2)}, u32[]{:S(2)}) async-start(f32[128,8,128]{2,1,0:T(8,128)} %copy-done.1), calls=%async_computation.1 | async-start | bytes 1048576 | tf_op jit(solution)/shard_map/all_to_all | solution.py:347
  62.0 5.8 %collective-permute-start.9 = (f32[1024,128]{1,0:T(8,128)S(1)}, f32[1024,128]{1,0:T(8,128)S(1)}, u32[]{:S(2)}, u32[]{:S(2)}) collective-permute-start(f32[1024,128]{1,0:T(8,128)S(1)} %broadcast_select_fusion), channel_id=1, source_target_pairs={{0,4},{1,5},{2,6},{3,7},{4,0},{5,1},{6,2},{7,3},{8,12},{9,13},{10,... | collective-permute-start | bytes 1572872 | tf_op jit(solution)/shard_map/ppermute | solution.py:343
  62.2 1.9 %collective-permute-start = (f32[168,128]{1,0:T(8,128)S(1)}, f32[168,128]{1,0:T(8,128)S(1)}, u32[]{:S(2)}, u32[]{:S(2)}) collective-permute-start(f32[168,128]{1,0:T(8,128)S(1)} %get-tuple-element.26), channel_id=1, source_target_pairs={{0,4},{1,5},{2,6},{3,7},{4,0},{5,1},{6,2},{7,3},{8,12},{9,13},{10,... | collective-permute-start | bytes 258056 | tf_op jit(solution)/shard_map/ppermute | solution.py:343
  64.1 33.3 %copy-start.5 = (f32[2048]{0:T(1024)S(1)}, f32[2048]{0:T(1024)}, u32[]{:S(2)}) copy-start(f32[2048]{0:T(1024)} %param.13) | copy-start | bytes 24580
  64.1 10.3 %collective-permute-start.3 = (f32[168,128]{1,0:T(8,128)S(1)}, f32[168,128]{1,0:T(8,128)S(1)}, u32[]{:S(2)}, u32[]{:S(2)}) collective-permute-start(f32[168,128]{1,0:T(8,128)S(1)} %add.39), channel_id=1, source_target_pairs={{0,96},{1,97},{2,98},{3,99},{4,100},{5,101},{6,102},{7,103},{8,104... | collective-permute-start | bytes 258056 | tf_op jit(solution)/shard_map/ppermute | solution.py:334
  65.0 9.4 %collective-permute-start.2 = (f32[168,128]{1,0:T(8,128)S(1)}, f32[168,128]{1,0:T(8,128)S(1)}, u32[]{:S(2)}, u32[]{:S(2)}) collective-permute-start(f32[168,128]{1,0:T(8,128)S(1)} %add.39), channel_id=1, source_target_pairs={{0,32},{1,33},{2,34},{3,35},{4,36},{5,37},{6,38},{7,39},{8,40},{9,... | collective-permute-start | bytes 258056 | tf_op jit(solution)/shard_map/ppermute | solution.py:334
  66.2 8.2 %collective-permute-start.1 = (f32[168,128]{1,0:T(8,128)S(1)}, f32[168,128]{1,0:T(8,128)S(1)}, u32[]{:S(2)}, u32[]{:S(2)}) collective-permute-start(f32[168,128]{1,0:T(8,128)S(1)} %add.39), channel_id=1, source_target_pairs={{0,64},{1,65},{2,66},{3,67},{4,68},{5,69},{6,70},{7,71},{8,72},{9,... | collective-permute-start | bytes 258056 | tf_op jit(solution)/shard_map/ppermute | solution.py:334
  68.6 28.8 %all-to-all-start.2 = ((f32[64,16,128]{2,1,0:T(8,128)}), f32[64,16,128]{2,1,0:T(8,128)S(1)}, u32[]{:S(2)}, u32[]{:S(2)}) async-start(f32[64,16,128]{2,1,0:T(8,128)} %bitcast.6), calls=%async_computation.2 | async-start | bytes 1048576 | tf_op jit(solution)/shard_map/all_to_all | solution.py:347
  74.5 9.5 %collective-permute-start.6 = (f32[168,128]{1,0:T(8,128)S(1)}, f32[168,128]{1,0:T(8,128)S(1)}, u32[]{:S(2)}, u32[]{:S(2)}) collective-permute-start(f32[168,128]{1,0:T(8,128)S(1)} %add_add_fusion.1), channel_id=1, source_target_pairs={{0,24},{1,25},{2,26},{3,27},{4,28},{5,29},{6,30},{7,31},{8,0},{9,1... | collective-permute-start | bytes 258056 | tf_op jit(solution)/shard_map/ppermute | solution.py:334
  77.3 8.7 %collective-permute-start.5 = (f32[168,128]{1,0:T(8,128)S(1)}, f32[168,128]{1,0:T(8,128)S(1)}, u32[]{:S(2)}, u32[]{:S(2)}) collective-permute-start(f32[168,128]{1,0:T(8,128)S(1)} %add_add_fusion.1), channel_id=1, source_target_pairs={{0,8},{1,9},{2,10},{3,11},{4,12},{5,13},{6,14},{7,15},{8,16},{9,17... | collective-permute-start | bytes 258056 | tf_op jit(solution)/shard_map/ppermute | solution.py:334
  77.3 9.7 %collective-permute-start.4 = (f32[168,128]{1,0:T(8,128)S(1)}, f32[168,128]{1,0:T(8,128)S(1)}, u32[]{:S(2)}, u32[]{:S(2)}) collective-permute-start(f32[168,128]{1,0:T(8,128)S(1)} %add_add_fusion.1), channel_id=1, source_target_pairs={{0,16},{1,17},{2,18},{3,19},{4,20},{5,21},{6,22},{7,23},{8,24},{9,... | collective-permute-start | bytes 258056 | tf_op jit(solution)/shard_map/ppermute | solution.py:334
  87.0 4.6 %collective-permute-start.7 = (f32[168,128]{1,0:T(8,128)S(1)}, f32[168,128]{1,0:T(8,128)S(1)}, u32[]{:S(2)}, u32[]{:S(2)}) collective-permute-start(f32[168,128]{1,0:T(8,128)S(1)} %add_add_fusion), channel_id=1, source_target_pairs={{0,1},{1,0},{2,3},{3,2},{4,5},{5,4},{6,7},{7,6},{8,9},{9,8},{10,11... | collective-permute-start | bytes 258056 | tf_op jit(solution)/shard_map/ppermute | solution.py:390
  91.6 5.8 %collective-permute-start.8 = (f32[168,128]{1,0:T(8,128)S(1)}, f32[168,128]{1,0:T(8,128)S(1)}, u32[]{:S(2)}, u32[]{:S(2)}) collective-permute-start(f32[168,128]{1,0:T(8,128)S(1)} %add.46.first), channel_id=1, source_target_pairs={{0,3},{1,2},{2,1},{3,0},{4,7},{5,6},{6,5},{7,4},{8,11},{9,10},{10,... | collective-permute-start | bytes 258056 | tf_op jit(solution)/shard_map/ppermute | solution.py:391
